TPU v7x, 32 devices: a whole 2x2x4 slice. The times are simulated.
32 devices in a mesh: win: 8 (over z, y), seq: 4 (over x, core).
Axes of the slice: x: 2, y: 2, z: 4, core: 2. Of those that a mesh axis runs over, the one named last changes fastest.
Arguments:
- queries: bfloat16 [2, 8, 2048, 2048], P(None, 'win', 'seq'), may hold values from -4.5 to 4.5
- key_states: bfloat16 [2, 8, 2048, 2048], P(None, 'win', 'seq'), may hold values from -4.5 to 4.5
- value_states: bfloat16 [2, 8, 2048, 2048], P(None, 'win', 'seq'), may hold values from -5 to 5
- out_grad: bfloat16 [2, 8, 2048, 2048], P(None, 'win', 'seq'), may hold values from -60 to 60
Outputs:
- query_grad: bfloat16 [2, 8, 2048, 2048], P(None, 'win', 'seq')
- key_grad: bfloat16 [2, 8, 2048, 2048], P(None, 'win', 'seq')
- value_grad: bfloat16 [2, 8, 2048, 2048], P(None, 'win', 'seq')
All inputs are finite; a program needn't handle non-finite values.
Results may differ from a plain program's by a relative error of at most 0.0095.
Values may be sent and summed in bfloat16 or wider, within the bound.
No kernel may reach another device: no remote copies, remote signals or barrier semaphores. Data moves between devices by JAX's collectives and lax.ppermute only.
A program may use at most 192 MiB of HBM per device.

v0:
```python
import functools
import math

import jax
import jax.numpy as jnp
from jax import lax
from jax.experimental import pallas as pl
from jax.experimental.pallas import tpu as pltpu
from jax.sharding import PartitionSpec as P


HDIM = 128
COLS = 64
HALF = COLS // 2
UNITS = 2


def exchanged(block, across, west):
    wins, seqs = lax.axis_size("win"), lax.axis_size("seq")
    route = [
        (w * seqs + s, ((w - west) % wins) * seqs + (s ^ across))
        for w in range(wins)
        for s in range(seqs)
    ]
    return lax.ppermute(block, ("win", "seq"), route)


def cost(flops, read, exps=0):
    return pl.CostEstimate(flops=int(flops), bytes_accessed=int(read), transcendentals=int(exps))


def packed(arrays, me, sample, first, units, heads_each, peers):
    rows = arrays[0][0].shape[2]
    width = units * HDIM
    share, offset = heads_each // units, first // units
    sizes = [rows * (COLS if half is None else HALF) for _, half in arrays]
    count = len(arrays)

    def kernel(me_ref, *refs):
        for i in range(len(peers)):
            out, at = refs[i - len(peers)], 0
            for piece, size in zip(refs[i * count :], sizes):
                out[at : at + size] = piece[0, 0].reshape(size, width)
                at += size

    specs = [
        pl.BlockSpec(
            (1, 1, rows, COLS if half is None else HALF, width),
            lambda u, m, k=k, half=half: (sample, 0, 0, half or 0, (m[0] ^ k) * share + offset),
        )
        for k in peers
        for _, half in arrays
    ]
    out = pl.pallas_call(
        kernel,
        grid_spec=pltpu.PrefetchScalarGridSpec(
            num_scalar_prefetch=1,
            grid=(1,),
            in_specs=specs,
            out_specs=[pl.BlockSpec((sum(sizes), width), lambda u, m: (0, 0))] * len(peers),
        ),
        out_shape=[jax.ShapeDtypeStruct((sum(sizes), width), jnp.bfloat16)] * len(peers),
        name="pack",
        cost_estimate=cost(0, 4 * sum(sizes) * width * len(peers)),
    )(me, *[a for _ in peers for a, _ in arrays])
    return dict(zip(peers, out))


def window_grads(args, me, sample, first, units, heads_each, seqs, arrived, arrived_west):
    rows = args[0].shape[2]
    tokens, part = rows * COLS, rows * HALF
    total = tokens * seqs
    block, slab = min(512, total), min(256, total)
    turned = seqs // 2
    here = [k for k in range(seqs) if k]
    factor = HDIM ** (-0.5)
    slope = factor * math.log2(math.e)

    def product(a, b, i, j):
        return lax.dot_general(a, b, (((i,), (j,)), ((), ())), preferred_element_type=jnp.float32)

    def folded(reduce, x):
        return reduce(x.reshape(-1, 8, x.shape[1]), axis=0)

    def kernel(me_ref, q_own, k_own, v_own, g_own, *refs):
        got = refs[: len(here)]
        got_west = refs[len(here) : len(here) + seqs]
        outs = refs[-8 - 2 * seqs : -8]
        qs, ks, vs, gs, kt, dq, dk, dv = refs[-8:]

        for n, (own, held) in enumerate(((q_own, qs), (k_own, ks), (v_own, vs))):
            held[0:tokens] = own[0, 0].reshape(tokens, HDIM)
            for i, k in enumerate(here):
                held[k * tokens : (k + 1) * tokens] = got[i][n * tokens : (n + 1) * tokens]
        for k in range(seqs):
            near = g_own[0, 0] if k == 0 else got[k - 1][3 * tokens :].reshape(rows, HALF, HDIM)
            far = got_west[k][...].reshape(rows, HALF, HDIM)
            at = (k ^ turned) * tokens
            gs[at : at + tokens] = jnp.concatenate([near, far], axis=1).reshape(tokens, HDIM)
        kt[...] = ks[...].T
        dk[...] = jnp.zeros_like(dk)
        dv[...] = jnp.zeros_like(dv)

        def step(i, carry):
            at = pl.ds(pl.multiple_of(i * block, block), block)
            query, grad = qs[at, :], gs[at, :]
            slabs = [slice(j, j + slab) for j in range(0, total, slab)]
            scores = [product(ks[j, :], query, 1, 1) for j in slabs]
            top = functools.reduce(jnp.maximum, [folded(jnp.max, x) for x in scores])
            top = jnp.max(top, axis=0, keepdims=True) * slope
            weights = [jnp.exp2(x * slope - top) for x in scores]
            grad_probs = [product(vs[j, :], grad, 1, 1) for j in slabs]
            mass = sum(folded(jnp.sum, w) for w in weights)
            dots = sum(folded(jnp.sum, w * g) for w, g in zip(weights, grad_probs))
            scale = 1.0 / jnp.sum(mass, axis=0, keepdims=True)
            row_dot = jnp.sum(dots, axis=0, keepdims=True) * scale
            column = scale.T
            grad = (grad.astype(jnp.float32) * column).astype(jnp.bfloat16)
            query = (query.astype(jnp.float32) * (column * factor)).astype(jnp.bfloat16)
            turned_grad = 0.0
            for j, w, g in zip(slabs, weights, grad_probs):
                dv[j, :] += product(w.astype(jnp.bfloat16), grad, 1, 0)
                u = (w * (g - row_dot)).astype(jnp.bfloat16)
                dk[j, :] += product(u, query, 1, 0)
                turned_grad += product(kt[:, j], u, 1, 0)
            dq[at, :] = (turned_grad * (scale * factor)).T.astype(jnp.bfloat16)
            return carry

        lax.fori_loop(0, total // block, step, 0)

        for k in range(seqs):
            at = pl.ds((k ^ turned) * tokens, tokens)
            for n, held in enumerate((dq, dk, dv)):
                value = held[at, :]
                value = value.astype(jnp.bfloat16).reshape(rows, COLS, HDIM)
                to = pl.ds(n * part, part)
                outs[k][to, :] = value[:, :HALF].reshape(part, HDIM)
                outs[seqs + k][to, :] = value[:, HALF:].reshape(part, HDIM)

    own = [
        pl.BlockSpec(
            (1, 1, rows, COLS, HDIM), lambda u, m: (sample, 0, 0, 0, m[0] * heads_each + first + u)
        )
    ] * 3 + [
        pl.BlockSpec(
            (1, 1, rows, HALF, HDIM), lambda u, m: (sample, 0, 0, 1, m[0] * heads_each + first + u)
        )
    ]
    full, small = 3 * tokens + part, part
    got = [pl.BlockSpec((full, HDIM), lambda u, m: (0, u))] * len(here)
    got_west = [pl.BlockSpec((small, HDIM), lambda u, m: (0, first + u))] * seqs
    out_rows = 3 * part
    held = pltpu.VMEM((total, HDIM), jnp.bfloat16)
    wide = pltpu.VMEM((total, HDIM), jnp.float32)
    out = pl.pallas_call(
        kernel,
        grid_spec=pltpu.PrefetchScalarGridSpec(
            num_scalar_prefetch=1,
            grid=(units,),
            in_specs=own + got + got_west,
            out_specs=[pl.BlockSpec((out_rows, HDIM), lambda u, m: (0, u))] * (2 * seqs),
            scratch_shapes=[held] * 4
            + [pltpu.VMEM((HDIM, total), jnp.bfloat16), held, wide, wide],
        ),
        out_shape=[jax.ShapeDtypeStruct((out_rows, units * HDIM), jnp.bfloat16)] * (2 * seqs),
        compiler_params=pltpu.CompilerParams(vmem_limit_bytes=48 * 2**20),
        name="grads",
        cost_estimate=cost(
            units * 10 * total * total * HDIM, units * 14 * total * HDIM, units * total * total
        ),
    )(
        me,
        *args,
        *[arrived[k] for k in here],
        *[arrived_west[k] for k in range(seqs)],
    )
    return out[:seqs], out[seqs:]


def placed(results, me, shape, sample, first, units, heads_each, pieces):
    rows = shape[2]
    width = units * HDIM
    share, offset = heads_each // units, first // units

    def kernel(me_ref, *refs):
        outs, sems = refs[-4:-1], refs[-1]
        copies = []
        for i, (k, column, _) in enumerate(pieces):
            head = pl.multiple_of(((me_ref[0] ^ k) * share + offset) * width, width)
            for n in range(3):
                to = outs[n].at[sample, 0, :, pl.ds(column, HALF), pl.ds(head, width)]
                copies.append(pltpu.make_async_copy(refs[i].at[n], to, sems.at[i, n]))
        for copy in copies:
            copy.start()
        for copy in copies:
            copy.wait()

    block = (3, rows, HALF, width)
    kept = [pl.BlockSpec(memory_space=pl.ANY)] * len(results)
    return pl.pallas_call(
        kernel,
        grid_spec=pltpu.PrefetchScalarGridSpec(
            num_scalar_prefetch=1,
            grid=(1,),
            in_specs=[pl.BlockSpec(block, lambda k, m: (0, 0, 0, 0))] * len(pieces) + kept,
            out_specs=[pl.BlockSpec(memory_space=pl.ANY)] * 3,
            scratch_shapes=[pltpu.SemaphoreType.DMA((len(pieces), 3))],
        ),
        out_shape=[jax.ShapeDtypeStruct(shape, jnp.bfloat16)] * 3,
        input_output_aliases={1 + len(pieces) + i: i for i in range(len(results))},
        name="place",
        cost_estimate=cost(0, 4 * math.prod(block) * len(pieces)),
    )(me, *[x.reshape(block) for _, _, x in pieces], *results)


def on_device(*args):
    samples, _, local_tokens, model_width = args[0].shape
    seqs = lax.axis_size("seq")
    heads_each = model_width // HDIM // seqs
    rows = local_tokens // COLS
    me = lax.axis_index("seq").astype(jnp.int32).reshape(1)
    args = [a.reshape(samples, 1, rows, COLS, model_width) for a in args]
    shape = args[0].shape
    turned = seqs // 2
    crossing, beside = list(range(turned, seqs)), list(range(turned))
    units = math.gcd(UNITS, heads_each)
    chunks = [(n, f) for n in range(samples) for f in range(0, heads_each, units)]

    near = [(args[0], None), (args[1], None), (args[2], None), (args[3], 1)]
    moving, got_west, step = [], {}, 0

    def sent(arrays, place, peers, west):
        nonlocal step
        step += 1
        blocks = packed(arrays, me, *place, peers)
        return {k: exchanged(blocks[k], k, west) for k in peers}

    for sample, first in chunks:
        at = (sample, first, units, heads_each)
        got = {}
        if not moving:
            for k in crossing:
                got.update(sent(near, at, [k], 0))
        else:
            got.update(sent(near, at, crossing + beside[1:], 0))
        if sample not in got_west:
            whole = (sample, 0, heads_each, heads_each)
            got_west[sample] = sent([(args[3], 0)], whole, beside + crossing, 1)
        if not moving and beside[1:]:
            got.update(sent(near, at, beside[1:], 0))
        moving.append(got)
    leaving = []
    for (sample, first), got in zip(chunks, moving):
        stay, east = window_grads(
            args, me, sample, first, units, heads_each, seqs, got, got_west[sample]
        )
        came = {k: exchanged(east[k], k, -1) for k in crossing + beside}
        stayed = {k: exchanged(stay[k], k, 0) if k else stay[k] for k in crossing + beside}
        leaving.append((stayed, came))
    results = []
    for i, ((sample, first), (stayed, came)) in enumerate(zip(chunks, leaving)):
        early = [(k, HALF, stayed[k]) for k in beside] + [(k, 0, came[k]) for k in beside]
        late = [(k, 0, came[k]) for k in crossing]
        last = [(k, HALF, stayed[k]) for k in crossing]
        for pieces in [early, late, last] if i == len(chunks) - 1 else [early + late + last]:
            results = placed(results, me, shape, sample, first, units, heads_each, pieces)
    return tuple(r.reshape(samples, 1, local_tokens, model_width) for r in results)


def solution(mesh):
    spec = P(None, "win", "seq", None)

    return jax.shard_map(
        on_device,
        mesh=mesh,
        in_specs=(spec,) * 4,
        out_specs=(spec,) * 3,
        check_vma=False,
    )
```

profile of v0, /device:TPU:0, one launch (start us, length us, event | category | flops | bytes accessed | tf_op | source)
XLA Modules:
  0.0 420.1 jit_solution(9022186056091458852)
XLA Ops:
  10.1 4.6 %collective-permute-start.27 = (bf16[256,512]{1,0:T(8,128)(2,1)}, bf16[256,512]{1,0:T(8,128)(2,1)S(1)}, u32[]{:S(2)}, u32[]{:S(2)}) collective-permute-start(bf16[256,512]{1,0:T(8,128)(2,1)} %get-tuple-element.99), channel_id=1, source_target_pairs={{0,28},{1,29},{2,30},{3,31},{4,0},{5,1},{6,2},{7,3},{8,4},{9,5},{1... | collective-permute-start | bytes 786440 | tf_op jit(solution)/shard_map/ppermute | solution.py:25
  30.9 5.6 %collective-permute-done.29.refs_5_ = bf16[256,512]{1,0:T(8,128)(2,1)S(1)} collective-permute-done((bf16[256,512]{1,0:T(8,128)(2,1)}, bf16[256,512]{1,0:T(8,128)(2,1)S(1)}, u32[]{:S(2)}, u32[]{:S(2)}) %collective-permute-start.29) | collective-permute-done | bytes 262176 | tf_op jit(solution)/shard_map/ppermute | solution.py:25
  44.9 8.0 %collective-permute-done.3.refs_3_ = bf16[256,512]{1,0:T(8,128)(2,1)S(1)} collective-permute-done((bf16[256,512]{1,0:T(8,128)(2,1)}, bf16[256,512]{1,0:T(8,128)(2,1)S(1)}, u32[]{:S(2)}, u32[]{:S(2)}) %collective-permute-start.3) | collective-permute-done | bytes 262176 | tf_op jit(solution)/shard_map/ppermute | solution.py:25
  64.8 3.6 collective-permute-start.24
  74.6 8.6 %collective-permute-done.40.refs_2_ = bf16[1792,256]{1,0:T(8,128)(2,1)} collective-permute-done((bf16[1792,256]{1,0:T(8,128)(2,1)}, bf16[1792,256]{1,0:T(8,128)(2,1)}, u32[]{:S(2)}, u32[]{:S(2)}) %collective-permute-start.40) | collective-permute-done | bytes 917536 | tf_op jit(solution)/shard_map/ppermute | solution.py:25
  83.1 8.1 %collective-permute-start.15 = (bf16[1792,256]{1,0:T(8,128)(2,1)}, bf16[1792,256]{1,0:T(8,128)(2,1)S(1)}, u32[]{:S(2)}, u32[]{:S(2)}) collective-permute-start(bf16[1792,256]{1,0:T(8,128)(2,1)} %get-tuple-element.86), channel_id=1, source_target_pairs={{0,2},{1,3},{2,0},{3,1},{4,6},{5,7},{6,4},{7,5},{8,10},{9,11},{10,... | collective-permute-start | bytes 2752520 | tf_op jit(solution)/shard_map/ppermute | solution.py:25
  91.2 18.2 %collective-permute-done.25.refs_1_ = bf16[1792,256]{1,0:T(8,128)(2,1)} collective-permute-done((bf16[1792,256]{1,0:T(8,128)(2,1)}, bf16[1792,256]{1,0:T(8,128)(2,1)}, u32[]{:S(2)}, u32[]{:S(2)}) %collective-permute-start.25) | collective-permute-done | bytes 917536 | tf_op jit(solution)/shard_map/ppermute | solution.py:25
  109.4 13.0 %collective-permute-done.26.refs_2_ = bf16[1792,256]{1,0:T(8,128)(2,1)} collective-permute-done((bf16[1792,256]{1,0:T(8,128)(2,1)}, bf16[1792,256]{1,0:T(8,128)(2,1)}, u32[]{:S(2)}, u32[]{:S(2)}) %collective-permute-start.26) | collective-permute-done | bytes 917536 | tf_op jit(solution)/shard_map/ppermute | solution.py:25
  122.4 8.1 %collective-permute-start.1 = (bf16[1792,256]{1,0:T(8,128)(2,1)}, bf16[1792,256]{1,0:T(8,128)(2,1)S(1)}, u32[]{:S(2)}, u32[]{:S(2)}) collective-permute-start(bf16[1792,256]{1,0:T(8,128)(2,1)} %get-tuple-element.71), channel_id=1, source_target_pairs={{0,2},{1,3},{2,0},{3,1},{4,6},{5,7},{6,4},{7,5},{8,10},{9,11},{10,... | collective-permute-start | bytes 2752520 | tf_op jit(solution)/shard_map/ppermute | solution.py:25
  134.3 36.7 %grads.7 = (bf16[768,256]{1,0:T(8,128)(2,1)S(1)}, bf16[768,256]{1,0:T(8,128)(2,1)S(1)}, bf16[768,256]{1,0:T(8,128)(2,1)S(1)}, bf16[768,256]{1,0:T(8,128)(2,1)S(1...) custom-call(s32[1]{0:T(128)} %bitcast.me_ref, ...), custom_call_target="tpu_custom_call" | custom-call | flops 10737418240 | bytes 7340032 | tf_op jit(solution)/shard_map/grads/pallas_call | solution.py:155
  172.9 15.0 %collective-permute-done.1.refs_1_ = bf16[1792,256]{1,0:T(8,128)(2,1)S(1)} collective-permute-done((bf16[1792,256]{1,0:T(8,128)(2,1)}, bf16[1792,256]{1,0:T(8,128)(2,1)S(1)}, u32[]{:S(2)}, u32[]{:S(2)}) %collective-permute-start.1) | collective-permute-done | bytes 917536 | tf_op jit(solution)/shard_map/ppermute | solution.py:25
  188.0 13.0 %collective-permute-done.2.refs_2_ = bf16[1792,256]{1,0:T(8,128)(2,1)S(1)} collective-permute-done((bf16[1792,256]{1,0:T(8,128)(2,1)}, bf16[1792,256]{1,0:T(8,128)(2,1)S(1)}, u32[]{:S(2)}, u32[]{:S(2)}) %collective-permute-start.2) | collective-permute-done | bytes 917536 | tf_op jit(solution)/shard_map/ppermute | solution.py:25
  201.9 11.8 %collective-permute-start.45 = (bf16[768,256]{1,0:T(8,128)(2,1)S(1)}, bf16[768,256]{1,0:T(8,128)(2,1)S(1)}, u32[]{:S(2)}, u32[]{:S(2)}) collective-permute-start(bf16[768,256]{1,0:T(8,128)(2,1)S(1)} %get-tuple-element.116), channel_id=1, source_target_pairs={{0,7},{1,6},{2,5},{3,4},{4,11},{5,10},{6,9},{7,8},{8,15},{9,14},{1... | collective-permute-start | bytes 1179656 | tf_op jit(solution)/shard_map/ppermute | solution.py:25
  215.3 36.8 %grads.6 = (bf16[768,256]{1,0:T(8,128)(2,1)S(1)}, bf16[768,256]{1,0:T(8,128)(2,1)S(1)}, bf16[768,256]{1,0:T(8,128)(2,1)S(1)}, bf16[768,256]{1,0:T(8,128)(2,1)S(1...) custom-call(s32[1]{0:T(128)} %bitcast.me_ref, ...), custom_call_target="tpu_custom_call" | custom-call | flops 10737418240 | bytes 7340032 | tf_op jit(solution)/shard_map/grads/pallas_call | solution.py:155
  254.1 36.5 %grads.5 = (bf16[768,256]{1,0:T(8,128)(2,1)S(1)}, bf16[768,256]{1,0:T(8,128)(2,1)S(1)}, bf16[768,256]{1,0:T(8,128)(2,1)S(1)}, bf16[768,256]{1,0:T(8,128)(2,1)S(1...) custom-call(s32[1]{0:T(128)} %bitcast.me_ref, ...), custom_call_target="tpu_custom_call" | custom-call | flops 10737418240 | bytes 7340032 | tf_op jit(solution)/shard_map/grads/pallas_call | solution.py:155
  296.4 14.1 %collective-permute-done.35 = bf16[768,256]{1,0:T(8,128)(2,1)S(1)} collective-permute-done((bf16[768,256]{1,0:T(8,128)(2,1)S(1)}, bf16[768,256]{1,0:T(8,128)(2,1)S(1)}, u32[]{:S(2)}, u32[]{:S(2)}) %collective-permute-start.35) | collective-permute-done | bytes 393248 | tf_op jit(solution)/shard_map/ppermute | solution.py:25
  316.6 4.3 %collective-permute-done.37 = bf16[768,256]{1,0:T(8,128)(2,1)S(1)} collective-permute-done((bf16[768,256]{1,0:T(8,128)(2,1)S(1)}, bf16[768,256]{1,0:T(8,128)(2,1)S(1)}, u32[]{:S(2)}, u32[]{:S(2)}) %collective-permute-start.37) | collective-permute-done | bytes 393248 | tf_op jit(solution)/shard_map/ppermute | solution.py:25
  320.9 5.8 %collective-permute-start.21 = (bf16[768,256]{1,0:T(8,128)(2,1)S(1)}, bf16[768,256]{1,0:T(8,128)(2,1)S(1)}, u32[]{:S(2)}, u32[]{:S(2)}) collective-permute-start(bf16[768,256]{1,0:T(8,128)(2,1)S(1)} %get-tuple-element.93), channel_id=1, source_target_pairs={{0,7},{1,6},{2,5},{3,4},{4,11},{5,10},{6,9},{7,8},{8,15},{9,14},{1... | collective-permute-start | bytes 1179656 | tf_op jit(solution)/shard_map/ppermute | solution.py:25
  330.0 36.5 %grads.4 = (bf16[768,256]{1,0:T(8,128)(2,1)S(1)}, bf16[768,256]{1,0:T(8,128)(2,1)S(1)}, bf16[768,256]{1,0:T(8,128)(2,1)S(1)}, bf16[768,256]{1,0:T(8,128)(2,1)S(1...) custom-call(s32[1]{0:T(128)} %bitcast.me_ref, ...), custom_call_target="tpu_custom_call" | custom-call | flops 10737418240 | bytes 7340032 | tf_op jit(solution)/shard_map/grads/pallas_call | solution.py:155
  367.4 7.5 %collective-permute-start.12 = (bf16[768,256]{1,0:T(8,128)(2,1)S(1)}, bf16[768,256]{1,0:T(8,128)(2,1)S(1)}, u32[]{:S(2)}, u32[]{:S(2)}) collective-permute-start(bf16[768,256]{1,0:T(8,128)(2,1)S(1)} %get-tuple-element.83), channel_id=1, source_target_pairs={{0,4},{1,5},{2,6},{3,7},{4,8},{5,9},{6,10},{7,11},{8,12},{9,13},{1... | collective-permute-start | bytes 1179656 | tf_op jit(solution)/shard_map/ppermute | solution.py:25
  377.7 23.5 %collective-permute-done.12 = bf16[768,256]{1,0:T(8,128)(2,1)S(1)} collective-permute-done((bf16[768,256]{1,0:T(8,128)(2,1)S(1)}, bf16[768,256]{1,0:T(8,128)(2,1)S(1)}, u32[]{:S(2)}, u32[]{:S(2)}) %collective-permute-start.12) | collective-permute-done | bytes 393248 | tf_op jit(solution)/shard_map/ppermute | solution.py:25
  401.3 3.8 place.6
  405.1 3.7 place.7
  408.8 3.7 place.8
  (178 shorter events, 88.3 us)
Async XLA Ops:
  2.8 66.3 %collective-permute-start.38 = (bf16[1792,256]{1,0:T(8,128)(2,1)}, bf16[1792,256]{1,0:T(8,128)(2,1)S(1)}, u32[]{:S(2)}, u32[]{:S(2)}) collective-permute-start(bf16[1792,256]{1,0:T(8,128)(2,1)} %pack.13), channel_id=1, source_target_pairs={{0,1},{1,0},{2,3},{3,2},{4,5},{5,4},{6,7},{7,6},{8,9},{9,8},{10,11... | collective-permute-start | bytes 2752520 | tf_op jit(solution)/shard_map/ppermute | solution.py:25
  5.4 65.0 %collective-permute-start.39 = (bf16[1792,256]{1,0:T(8,128)(2,1)}, bf16[1792,256]{1,0:T(8,128)(2,1)S(1)}, u32[]{:S(2)}, u32[]{:S(2)}) collective-permute-start(bf16[1792,256]{1,0:T(8,128)(2,1)} %pack.14), channel_id=1, source_target_pairs={{0,2},{1,3},{2,0},{3,1},{4,6},{5,7},{6,4},{7,5},{8,10},{9,11},{10,... | collective-permute-start | bytes 2752520 | tf_op jit(solution)/shard_map/ppermute | solution.py:25
  69.1 53.4 %collective-permute-start.26 = (bf16[1792,256]{1,0:T(8,128)(2,1)}, bf16[1792,256]{1,0:T(8,128)(2,1)}, u32[]{:S(2)}, u32[]{:S(2)}) collective-permute-start(bf16[1792,256]{1,0:T(8,128)(2,1)} %get-tuple-element.98), channel_id=1, source_target_pairs={{0,3},{1,2},{2,1},{3,0},{4,7},{5,6},{6,5},{7,4},{8,11},{9,10},{10,... | collective-permute-start | bytes 2752520 | tf_op jit(solution)/shard_map/ppermute | solution.py:25
  70.4 60.1 %collective-permute-start.14 = (bf16[1792,256]{1,0:T(8,128)(2,1)}, bf16[1792,256]{1,0:T(8,128)(2,1)S(1)}, u32[]{:S(2)}, u32[]{:S(2)}) collective-permute-start(bf16[1792,256]{1,0:T(8,128)(2,1)} %get-tuple-element.85), channel_id=1, source_target_pairs={{0,1},{1,0},{2,3},{3,2},{4,5},{5,4},{6,7},{7,6},{8,9},{9,8},{10,11... | collective-permute-start | bytes 2752520 | tf_op jit(solution)/shard_map/ppermute | solution.py:25
  83.1 88.7 %collective-permute-start.15 = (bf16[1792,256]{1,0:T(8,128)(2,1)}, bf16[1792,256]{1,0:T(8,128)(2,1)S(1)}, u32[]{:S(2)}, u32[]{:S(2)}) collective-permute-start(bf16[1792,256]{1,0:T(8,128)(2,1)} %get-tuple-element.86), channel_id=1, source_target_pairs={{0,2},{1,3},{2,0},{3,1},{4,6},{5,7},{6,4},{7,5},{8,10},{9,11},{10,... | collective-permute-start | bytes 2752520 | tf_op jit(solution)/shard_map/ppermute | solution.py:25
  91.2 80.7 %collective-permute-start.16 = (bf16[1792,256]{1,0:T(8,128)(2,1)}, bf16[1792,256]{1,0:T(8,128)(2,1)S(1)}, u32[]{:S(2)}, u32[]{:S(2)}) collective-permute-start(bf16[1792,256]{1,0:T(8,128)(2,1)} %get-tuple-element.87), channel_id=1, source_target_pairs={{0,3},{1,2},{2,1},{3,0},{4,7},{5,6},{6,5},{7,4},{8,11},{9,10},{10,... | collective-permute-start | bytes 2752520 | tf_op jit(solution)/shard_map/ppermute | solution.py:25
  109.4 63.5 %collective-permute-start = (bf16[1792,256]{1,0:T(8,128)(2,1)}, bf16[1792,256]{1,0:T(8,128)(2,1)S(1)}, u32[]{:S(2)}, u32[]{:S(2)}) collective-permute-start(bf16[1792,256]{1,0:T(8,128)(2,1)} %get-tuple-element.70), channel_id=1, source_target_pairs={{0,1},{1,0},{2,3},{3,2},{4,5},{5,4},{6,7},{7,6},{8,9},{9,8},{10,11... | collective-permute-start | bytes 2752520 | tf_op jit(solution)/shard_map/ppermute | solution.py:25
  122.4 65.5 %collective-permute-start.1 = (bf16[1792,256]{1,0:T(8,128)(2,1)}, bf16[1792,256]{1,0:T(8,128)(2,1)S(1)}, u32[]{:S(2)}, u32[]{:S(2)}) collective-permute-start(bf16[1792,256]{1,0:T(8,128)(2,1)} %get-tuple-element.71), channel_id=1, source_target_pairs={{0,2},{1,3},{2,0},{3,1},{4,6},{5,7},{6,4},{7,5},{8,10},{9,11},{10,... | collective-permute-start | bytes 2752520 | tf_op jit(solution)/shard_map/ppermute | solution.py:25
  130.5 70.5 %collective-permute-start.2 = (bf16[1792,256]{1,0:T(8,128)(2,1)}, bf16[1792,256]{1,0:T(8,128)(2,1)S(1)}, u32[]{:S(2)}, u32[]{:S(2)}) collective-permute-start(bf16[1792,256]{1,0:T(8,128)(2,1)} %get-tuple-element.72), channel_id=1, source_target_pairs={{0,3},{1,2},{2,1},{3,0},{4,7},{5,6},{6,5},{7,4},{8,11},{9,10},{10,... | collective-permute-start | bytes 2752520 | tf_op jit(solution)/shard_map/ppermute | solution.py:25
  171.8 41.9 %collective-permute-start.41 = (bf16[768,256]{1,0:T(8,128)(2,1)S(1)}, bf16[768,256]{1,0:T(8,128)(2,1)S(1)}, u32[]{:S(2)}, u32[]{:S(2)}) collective-permute-start(bf16[768,256]{1,0:T(8,128)(2,1)S(1)} %get-tuple-element.112), channel_id=1, source_target_pairs={{0,1},{1,0},{2,3},{3,2},{4,5},{5,4},{6,7},{7,6},{8,9},{9,8},{10,11... | collective-permute-start | bytes 1179656 | tf_op jit(solution)/shard_map/ppermute | solution.py:25
  172.9 79.9 %collective-permute-start.42 = (bf16[768,256]{1,0:T(8,128)(2,1)S(1)}, bf16[768,256]{1,0:T(8,128)(2,1)S(1)}, u32[]{:S(2)}, u32[]{:S(2)}) collective-permute-start(bf16[768,256]{1,0:T(8,128)(2,1)S(1)} %get-tuple-element.113), channel_id=1, source_target_pairs={{0,4},{1,5},{2,6},{3,7},{4,8},{5,9},{6,10},{7,11},{8,12},{9,13},{1... | collective-permute-start | bytes 1179656 | tf_op jit(solution)/shard_map/ppermute | solution.py:25
  172.9 79.9 %collective-permute-start.43 = (bf16[768,256]{1,0:T(8,128)(2,1)S(1)}, bf16[768,256]{1,0:T(8,128)(2,1)S(1)}, u32[]{:S(2)}, u32[]{:S(2)}) collective-permute-start(bf16[768,256]{1,0:T(8,128)(2,1)S(1)} %get-tuple-element.114), channel_id=1, source_target_pairs={{0,5},{1,4},{2,7},{3,6},{4,9},{5,8},{6,11},{7,10},{8,13},{9,12},{1... | collective-permute-start | bytes 1179656 | tf_op jit(solution)/shard_map/ppermute | solution.py:25
  188.0 65.5 %collective-permute-start.44 = (bf16[768,256]{1,0:T(8,128)(2,1)S(1)}, bf16[768,256]{1,0:T(8,128)(2,1)S(1)}, u32[]{:S(2)}, u32[]{:S(2)}) collective-permute-start(bf16[768,256]{1,0:T(8,128)(2,1)S(1)} %get-tuple-element.115), channel_id=1, source_target_pairs={{0,6},{1,7},{2,4},{3,5},{4,10},{5,11},{6,8},{7,9},{8,14},{9,15},{1... | collective-permute-start | bytes 1179656 | tf_op jit(solution)/shard_map/ppermute | solution.py:25
  201.9 51.6 %collective-permute-start.45 = (bf16[768,256]{1,0:T(8,128)(2,1)S(1)}, bf16[768,256]{1,0:T(8,128)(2,1)S(1)}, u32[]{:S(2)}, u32[]{:S(2)}) collective-permute-start(bf16[768,256]{1,0:T(8,128)(2,1)S(1)} %get-tuple-element.116), channel_id=1, source_target_pairs={{0,7},{1,6},{2,5},{3,4},{4,11},{5,10},{6,9},{7,8},{8,15},{9,14},{1... | collective-permute-start | bytes 1179656 | tf_op jit(solution)/shard_map/ppermute | solution.py:25
  252.9 41.2 %collective-permute-start.31 = (bf16[768,256]{1,0:T(8,128)(2,1)S(1)}, bf16[768,256]{1,0:T(8,128)(2,1)S(1)}, u32[]{:S(2)}, u32[]{:S(2)}) collective-permute-start(bf16[768,256]{1,0:T(8,128)(2,1)S(1)} %get-tuple-element.104), channel_id=1, source_target_pairs={{0,1},{1,0},{2,3},{3,2},{4,5},{5,4},{6,7},{7,6},{8,9},{9,8},{10,11... | collective-permute-start | bytes 1179656 | tf_op jit(solution)/shard_map/ppermute | solution.py:25
  253.5 41.8 %collective-permute-start.32 = (bf16[768,256]{1,0:T(8,128)(2,1)S(1)}, bf16[768,256]{1,0:T(8,128)(2,1)S(1)}, u32[]{:S(2)}, u32[]{:S(2)}) collective-permute-start(bf16[768,256]{1,0:T(8,128)(2,1)S(1)} %get-tuple-element.105), channel_id=1, source_target_pairs={{0,4},{1,5},{2,6},{3,7},{4,8},{5,9},{6,10},{7,11},{8,12},{9,13},{1... | collective-permute-start | bytes 1179656 | tf_op jit(solution)/shard_map/ppermute | solution.py:25
  253.5 42.0 %collective-permute-start.33 = (bf16[768,256]{1,0:T(8,128)(2,1)S(1)}, bf16[768,256]{1,0:T(8,128)(2,1)S(1)}, u32[]{:S(2)}, u32[]{:S(2)}) collective-permute-start(bf16[768,256]{1,0:T(8,128)(2,1)S(1)} %get-tuple-element.106), channel_id=1, source_target_pairs={{0,5},{1,4},{2,7},{3,6},{4,9},{5,8},{6,11},{7,10},{8,13},{9,12},{1... | collective-permute-start | bytes 1179656 | tf_op jit(solution)/shard_map/ppermute | solution.py:25
  253.6 42.6 %collective-permute-start.34 = (bf16[768,256]{1,0:T(8,128)(2,1)S(1)}, bf16[768,256]{1,0:T(8,128)(2,1)S(1)}, u32[]{:S(2)}, u32[]{:S(2)}) collective-permute-start(bf16[768,256]{1,0:T(8,128)(2,1)S(1)} %get-tuple-element.107), channel_id=1, source_target_pairs={{0,6},{1,7},{2,4},{3,5},{4,10},{5,11},{6,8},{7,9},{8,14},{9,15},{1... | collective-permute-start | bytes 1179656 | tf_op jit(solution)/shard_map/ppermute | solution.py:25
  310.5 56.8 %collective-permute-start.19 = (bf16[768,256]{1,0:T(8,128)(2,1)S(1)}, bf16[768,256]{1,0:T(8,128)(2,1)S(1)}, u32[]{:S(2)}, u32[]{:S(2)}) collective-permute-start(bf16[768,256]{1,0:T(8,128)(2,1)S(1)} %get-tuple-element.91), channel_id=1, source_target_pairs={{0,5},{1,4},{2,7},{3,6},{4,9},{5,8},{6,11},{7,10},{8,13},{9,12},{1... | collective-permute-start | bytes 1179656 | tf_op jit(solution)/shard_map/ppermute | solution.py:25
  313.7 53.7 %collective-permute-start.20 = (bf16[768,256]{1,0:T(8,128)(2,1)S(1)}, bf16[768,256]{1,0:T(8,128)(2,1)S(1)}, u32[]{:S(2)}, u32[]{:S(2)}) collective-permute-start(bf16[768,256]{1,0:T(8,128)(2,1)S(1)} %get-tuple-element.92), channel_id=1, source_target_pairs={{0,6},{1,7},{2,4},{3,5},{4,10},{5,11},{6,8},{7,9},{8,14},{9,15},{1... | collective-permute-start | bytes 1179656 | tf_op jit(solution)/shard_map/ppermute | solution.py:25
  320.9 54.0 %collective-permute-start.21 = (bf16[768,256]{1,0:T(8,128)(2,1)S(1)}, bf16[768,256]{1,0:T(8,128)(2,1)S(1)}, u32[]{:S(2)}, u32[]{:S(2)}) collective-permute-start(bf16[768,256]{1,0:T(8,128)(2,1)S(1)} %get-tuple-element.93), channel_id=1, source_target_pairs={{0,7},{1,6},{2,5},{3,4},{4,11},{5,10},{6,9},{7,8},{8,15},{9,14},{1... | collective-permute-start | bytes 1179656 | tf_op jit(solution)/shard_map/ppermute | solution.py:25
  326.7 48.2 %collective-permute-start.22 = (bf16[768,256]{1,0:T(8,128)(2,1)S(1)}, bf16[768,256]{1,0:T(8,128)(2,1)S(1)}, u32[]{:S(2)}, u32[]{:S(2)}) collective-permute-start(bf16[768,256]{1,0:T(8,128)(2,1)S(1)} %get-tuple-element.94), channel_id=1, source_target_pairs={{0,2},{1,3},{2,0},{3,1},{4,6},{5,7},{6,4},{7,5},{8,10},{9,11},{10,... | collective-permute-start | bytes 1179656 | tf_op jit(solution)/shard_map/ppermute | solution.py:25
  327.4 49.0 %collective-permute-start.23 = (bf16[768,256]{1,0:T(8,128)(2,1)S(1)}, bf16[768,256]{1,0:T(8,128)(2,1)S(1)}, u32[]{:S(2)}, u32[]{:S(2)}) collective-permute-start(bf16[768,256]{1,0:T(8,128)(2,1)S(1)} %get-tuple-element.95), channel_id=1, source_target_pairs={{0,3},{1,2},{2,1},{3,0},{4,7},{5,6},{6,5},{7,4},{8,11},{9,10},{10,... | collective-permute-start | bytes 1179656 | tf_op jit(solution)/shard_map/ppermute | solution.py:25
  376.4 41.5 %collective-permute-start.7 = (bf16[768,256]{1,0:T(8,128)(2,1)S(1)}, bf16[768,256]{1,0:T(8,128)(2,1)}, u32[]{:S(2)}, u32[]{:S(2)}) collective-permute-start(bf16[768,256]{1,0:T(8,128)(2,1)S(1)} %get-tuple-element.77), channel_id=1, source_target_pairs={{0,2},{1,3},{2,0},{3,1},{4,6},{5,7},{6,4},{7,5},{8,10},{9,11},{10,... | collective-permute-start | bytes 1179656 | tf_op jit(solution)/shard_map/ppermute | solution.py:25
  (68 other events, 1939.0 us)
where the time goes:
time: 422 us; the launch traced here: 420 us
  Pallas kernels  185 us (44%)
  waiting for transfers between devices  137 us (32%)
  starting transfers between devices  85.4 us (20%)
  local copies, waits for them, and re-layouts  11.6 us (3%)
    pallas_call x4, Pallas kernels, window_grads(): pl.pallas_call(kernel, grid_spec=pltpu.PrefetchScalarGridSpec(num_scalar_...  146 us
    ppermute x48, waiting for transfers between devices, exchanged(): return lax.ppermute(block, ('win', 'seq'), route)  137 us
    ppermute x48, starting transfers between devices, exchanged(): return lax.ppermute(block, ('win', 'seq'), route)  85.4 us
    pallas_call x8, Pallas kernels, packed(): pl.pallas_call(kernel, grid_spec=pltpu.PrefetchScalarGridSpec(num_scalar_...  20.9 us
    pallas_call x6, Pallas kernels, placed(): pl.pallas_call(kernel, grid_spec=pltpu.PrefetchScalarGridSpec(num_scalar_...  17.8 us
    unnamed x88, local copies, waits for them, and re-layouts  11.6 us
  transfers between devices with their start and end apart: 48, of which 15 were waited for; matrix products, arithmetic and copies ran while one was open for 0% of the time, Pallas kernels for 43%

commit v1 on v0

--- a/solution.py
+++ b/solution.py
@@ -177,7 +177,7 @@
     return out[:seqs], out[seqs:]
 
 
-def placed(results, me, shape, sample, first, units, heads_each, pieces):
+def placed(results, me, shape, sample, first, units, heads_each, pieces, direct):
     rows = shape[2]
     width = units * HDIM
     share, offset = heads_each // units, first // units
@@ -196,18 +196,21 @@
             copy.wait()
 
     block = (3, rows, HALF, width)
-    kept = [pl.BlockSpec(memory_space=pl.ANY)] * len(results)
+    kept_spec = pl.BlockSpec(memory_space=pl.ANY)
     return pl.pallas_call(
         kernel,
         grid_spec=pltpu.PrefetchScalarGridSpec(
             num_scalar_prefetch=1,
             grid=(1,),
-            in_specs=[pl.BlockSpec(block, lambda k, m: (0, 0, 0, 0))] * len(pieces) + kept,
+            in_specs=[kept_spec if direct else pl.BlockSpec(block, lambda k, m: (0, 0, 0, 0))]
+            * len(pieces)
+            + [kept_spec] * len(results),
             out_specs=[pl.BlockSpec(memory_space=pl.ANY)] * 3,
             scratch_shapes=[pltpu.SemaphoreType.DMA((len(pieces), 3))],
         ),
         out_shape=[jax.ShapeDtypeStruct(shape, jnp.bfloat16)] * 3,
         input_output_aliases={1 + len(pieces) + i: i for i in range(len(results))},
+        compiler_params=pltpu.CompilerParams(vmem_limit_bytes=2**20) if direct else None,
         name="place",
         cost_estimate=cost(0, 4 * math.prod(block) * len(pieces)),
     )(me, *[x.reshape(block) for _, _, x in pieces], *results)
@@ -263,7 +266,10 @@
         late = [(k, 0, came[k]) for k in crossing]
         last = [(k, HALF, stayed[k]) for k in crossing]
         for pieces in [early, late, last] if i == len(chunks) - 1 else [early + late + last]:
-            results = placed(results, me, shape, sample, first, units, heads_each, pieces)
+            direct = pieces is late or pieces is last
+            results = placed(
+                results, me, shape, sample, first, units, heads_each, pieces, direct
+            )
     return tuple(r.reshape(samples, 1, local_tokens, model_width) for r in results)
 
 

time: 422 us -> 422 us (level)
    unnamed x88 -> x98, local copies, waits for them, and re-layouts: 11.6 us -> 14.5 us
where the time goes in v1:
time: 422 us; the launch traced here: 421 us
  Pallas kernels  183 us (43%)
  waiting for transfers between devices  137 us (32%)
  starting transfers between devices  84.9 us (20%)
  local copies, waits for them, and re-layouts  14.5 us (3%)
    pallas_call x4, Pallas kernels, window_grads(): pl.pallas_call(kernel, grid_spec=pltpu.PrefetchScalarGridSpec(num_scalar_...  147 us
    ppermute x48, waiting for transfers between devices, exchanged(): return lax.ppermute(block, ('win', 'seq'), route)  137 us
    ppermute x48, starting transfers between devices, exchanged(): return lax.ppermute(block, ('win', 'seq'), route)  84.9 us
    pallas_call x8, Pallas kernels, packed(): pl.pallas_call(kernel, grid_spec=pltpu.PrefetchScalarGridSpec(num_scalar_...  21 us
    pallas_call x6, Pallas kernels, placed(): pl.pallas_call(kernel, grid_spec=pltpu.PrefetchScalarGridSpec(num_scalar_...  15.5 us
    unnamed x98, local copies, waits for them, and re-layouts  14.5 us
  transfers between devices with their start and end apart: 48, of which 15 were waited for; matrix products, arithmetic and copies ran while one was open for 0% of the time, Pallas kernels for 43%

profile of v1, /device:TPU:0, one launch (start us, length us, event | category | flops | bytes accessed | tf_op | source)
XLA Modules:
  0.0 420.7 jit_solution(12326243887932892546)
XLA Ops:
  10.1 4.6 %collective-permute-start.27 = (bf16[256,512]{1,0:T(8,128)(2,1)}, bf16[256,512]{1,0:T(8,128)(2,1)S(1)}, u32[]{:S(2)}, u32[]{:S(2)}) collective-permute-start(bf16[256,512]{1,0:T(8,128)(2,1)} %get-tuple-element.99), channel_id=1, source_target_pairs={{0,28},{1,29},{2,30},{3,31},{4,0},{5,1},{6,2},{7,3},{8,4},{9,5},{1... | collective-permute-start | bytes 786440 | tf_op jit(solution)/shard_map/ppermute | solution.py:25
  27.3 3.6 collective-permute-start.3
  30.9 5.6 %collective-permute-done.29.refs_5_ = bf16[256,512]{1,0:T(8,128)(2,1)S(1)} collective-permute-done((bf16[256,512]{1,0:T(8,128)(2,1)}, bf16[256,512]{1,0:T(8,128)(2,1)S(1)}, u32[]{:S(2)}, u32[]{:S(2)}) %collective-permute-start.29) | collective-permute-done | bytes 262176 | tf_op jit(solution)/shard_map/ppermute | solution.py:25
  44.9 8.0 %collective-permute-done.3.refs_3_ = bf16[256,512]{1,0:T(8,128)(2,1)S(1)} collective-permute-done((bf16[256,512]{1,0:T(8,128)(2,1)}, bf16[256,512]{1,0:T(8,128)(2,1)S(1)}, u32[]{:S(2)}, u32[]{:S(2)}) %collective-permute-start.3) | collective-permute-done | bytes 262176 | tf_op jit(solution)/shard_map/ppermute | solution.py:25
  74.6 8.6 %collective-permute-done.40.refs_2_ = bf16[1792,256]{1,0:T(8,128)(2,1)} collective-permute-done((bf16[1792,256]{1,0:T(8,128)(2,1)}, bf16[1792,256]{1,0:T(8,128)(2,1)}, u32[]{:S(2)}, u32[]{:S(2)}) %collective-permute-start.40) | collective-permute-done | bytes 917536 | tf_op jit(solution)/shard_map/ppermute | solution.py:25
  83.2 8.0 %collective-permute-start.15 = (bf16[1792,256]{1,0:T(8,128)(2,1)}, bf16[1792,256]{1,0:T(8,128)(2,1)S(1)}, u32[]{:S(2)}, u32[]{:S(2)}) collective-permute-start(bf16[1792,256]{1,0:T(8,128)(2,1)} %get-tuple-element.86), channel_id=1, source_target_pairs={{0,2},{1,3},{2,0},{3,1},{4,6},{5,7},{6,4},{7,5},{8,10},{9,11},{10,... | collective-permute-start | bytes 2752520 | tf_op jit(solution)/shard_map/ppermute | solution.py:25
  91.2 18.2 %collective-permute-done.25.refs_1_ = bf16[1792,256]{1,0:T(8,128)(2,1)} collective-permute-done((bf16[1792,256]{1,0:T(8,128)(2,1)}, bf16[1792,256]{1,0:T(8,128)(2,1)}, u32[]{:S(2)}, u32[]{:S(2)}) %collective-permute-start.25) | collective-permute-done | bytes 917536 | tf_op jit(solution)/shard_map/ppermute | solution.py:25
  109.4 13.1 %collective-permute-done.26.refs_2_ = bf16[1792,256]{1,0:T(8,128)(2,1)} collective-permute-done((bf16[1792,256]{1,0:T(8,128)(2,1)}, bf16[1792,256]{1,0:T(8,128)(2,1)}, u32[]{:S(2)}, u32[]{:S(2)}) %collective-permute-start.26) | collective-permute-done | bytes 917536 | tf_op jit(solution)/shard_map/ppermute | solution.py:25
  122.5 8.0 %collective-permute-start.1 = (bf16[1792,256]{1,0:T(8,128)(2,1)}, bf16[1792,256]{1,0:T(8,128)(2,1)S(1)}, u32[]{:S(2)}, u32[]{:S(2)}) collective-permute-start(bf16[1792,256]{1,0:T(8,128)(2,1)} %get-tuple-element.71), channel_id=1, source_target_pairs={{0,2},{1,3},{2,0},{3,1},{4,6},{5,7},{6,4},{7,5},{8,10},{9,11},{10,... | collective-permute-start | bytes 2752520 | tf_op jit(solution)/shard_map/ppermute | solution.py:25
  134.4 36.7 %grads.7 = (bf16[768,256]{1,0:T(8,128)(2,1)S(1)}, bf16[768,256]{1,0:T(8,128)(2,1)S(1)}, bf16[768,256]{1,0:T(8,128)(2,1)S(1)}, bf16[768,256]{1,0:T(8,128)(2,1)S(1...) custom-call(s32[1]{0:T(128)} %bitcast.me_ref, ...), custom_call_target="tpu_custom_call" | custom-call | flops 10737418240 | bytes 7340032 | tf_op jit(solution)/shard_map/grads/pallas_call | solution.py:155
  172.9 15.1 %collective-permute-done.1.refs_1_ = bf16[1792,256]{1,0:T(8,128)(2,1)S(1)} collective-permute-done((bf16[1792,256]{1,0:T(8,128)(2,1)}, bf16[1792,256]{1,0:T(8,128)(2,1)S(1)}, u32[]{:S(2)}, u32[]{:S(2)}) %collective-permute-start.1) | collective-permute-done | bytes 917536 | tf_op jit(solution)/shard_map/ppermute | solution.py:25
  188.0 13.1 %collective-permute-done.2.refs_2_ = bf16[1792,256]{1,0:T(8,128)(2,1)S(1)} collective-permute-done((bf16[1792,256]{1,0:T(8,128)(2,1)}, bf16[1792,256]{1,0:T(8,128)(2,1)S(1)}, u32[]{:S(2)}, u32[]{:S(2)}) %collective-permute-start.2) | collective-permute-done | bytes 917536 | tf_op jit(solution)/shard_map/ppermute | solution.py:25
  202.0 11.8 %collective-permute-start.45 = (bf16[768,256]{1,0:T(8,128)(2,1)S(1)}, bf16[768,256]{1,0:T(8,128)(2,1)S(1)}, u32[]{:S(2)}, u32[]{:S(2)}) collective-permute-start(bf16[768,256]{1,0:T(8,128)(2,1)S(1)} %get-tuple-element.116), channel_id=1, source_target_pairs={{0,7},{1,6},{2,5},{3,4},{4,11},{5,10},{6,9},{7,8},{8,15},{9,14},{1... | collective-permute-start | bytes 1179656 | tf_op jit(solution)/shard_map/ppermute | solution.py:25
  215.3 36.8 %grads.6 = (bf16[768,256]{1,0:T(8,128)(2,1)S(1)}, bf16[768,256]{1,0:T(8,128)(2,1)S(1)}, bf16[768,256]{1,0:T(8,128)(2,1)S(1)}, bf16[768,256]{1,0:T(8,128)(2,1)S(1...) custom-call(s32[1]{0:T(128)} %bitcast.me_ref, ...), custom_call_target="tpu_custom_call" | custom-call | flops 10737418240 | bytes 7340032 | tf_op jit(solution)/shard_map/grads/pallas_call | solution.py:155
  254.2 36.6 %grads.5 = (bf16[768,256]{1,0:T(8,128)(2,1)S(1)}, bf16[768,256]{1,0:T(8,128)(2,1)S(1)}, bf16[768,256]{1,0:T(8,128)(2,1)S(1)}, bf16[768,256]{1,0:T(8,128)(2,1)S(1...) custom-call(s32[1]{0:T(128)} %bitcast.me_ref, ...), custom_call_target="tpu_custom_call" | custom-call | flops 10737418240 | bytes 7340032 | tf_op jit(solution)/shard_map/grads/pallas_call | solution.py:155
  296.5 14.2 %collective-permute-done.35 = bf16[768,256]{1,0:T(8,128)(2,1)S(1)} collective-permute-done((bf16[768,256]{1,0:T(8,128)(2,1)S(1)}, bf16[768,256]{1,0:T(8,128)(2,1)S(1)}, u32[]{:S(2)}, u32[]{:S(2)}) %collective-permute-start.35) | collective-permute-done | bytes 393248 | tf_op jit(solution)/shard_map/ppermute | solution.py:25
  316.7 4.4 %collective-permute-done.37 = bf16[768,256]{1,0:T(8,128)(2,1)S(1)} collective-permute-done((bf16[768,256]{1,0:T(8,128)(2,1)S(1)}, bf16[768,256]{1,0:T(8,128)(2,1)S(1)}, u32[]{:S(2)}, u32[]{:S(2)}) %collective-permute-start.37) | collective-permute-done | bytes 393248 | tf_op jit(solution)/shard_map/ppermute | solution.py:25
  321.0 5.7 %collective-permute-start.21 = (bf16[768,256]{1,0:T(8,128)(2,1)S(1)}, bf16[768,256]{1,0:T(8,128)(2,1)S(1)}, u32[]{:S(2)}, u32[]{:S(2)}) collective-permute-start(bf16[768,256]{1,0:T(8,128)(2,1)S(1)} %get-tuple-element.93), channel_id=1, source_target_pairs={{0,7},{1,6},{2,5},{3,4},{4,11},{5,10},{6,9},{7,8},{8,15},{9,14},{1... | collective-permute-start | bytes 1179656 | tf_op jit(solution)/shard_map/ppermute | solution.py:25
  332.9 36.5 %grads.4 = (bf16[768,256]{1,0:T(8,128)(2,1)S(1)}, bf16[768,256]{1,0:T(8,128)(2,1)S(1)}, bf16[768,256]{1,0:T(8,128)(2,1)S(1)}, bf16[768,256]{1,0:T(8,128)(2,1)S(1...) custom-call(s32[1]{0:T(128)} %bitcast.me_ref, ...), custom_call_target="tpu_custom_call" | custom-call | flops 10737418240 | bytes 7340032 | tf_op jit(solution)/shard_map/grads/pallas_call | solution.py:155
  370.3 7.5 %collective-permute-start.12 = (bf16[768,256]{1,0:T(8,128)(2,1)S(1)}, bf16[768,256]{1,0:T(8,128)(2,1)S(1)}, u32[]{:S(2)}, u32[]{:S(2)}) collective-permute-start(bf16[768,256]{1,0:T(8,128)(2,1)S(1)} %get-tuple-element.83), channel_id=1, source_target_pairs={{0,4},{1,5},{2,6},{3,7},{4,8},{5,9},{6,10},{7,11},{8,12},{9,13},{1... | collective-permute-start | bytes 1179656 | tf_op jit(solution)/shard_map/ppermute | solution.py:25
  380.6 23.6 %collective-permute-done.12 = bf16[768,256]{1,0:T(8,128)(2,1)S(1)} collective-permute-done((bf16[768,256]{1,0:T(8,128)(2,1)S(1)}, bf16[768,256]{1,0:T(8,128)(2,1)S(1)}, u32[]{:S(2)}, u32[]{:S(2)}) %collective-permute-start.12) | collective-permute-done | bytes 393248 | tf_op jit(solution)/shard_map/ppermute | solution.py:25
  404.9 3.7 place.6
  408.6 3.7 place.7
  412.3 3.7 place.8
  (188 shorter events, 88.9 us)
Async XLA Ops:
  2.8 66.3 %collective-permute-start.38 = (bf16[1792,256]{1,0:T(8,128)(2,1)}, bf16[1792,256]{1,0:T(8,128)(2,1)S(1)}, u32[]{:S(2)}, u32[]{:S(2)}) collective-permute-start(bf16[1792,256]{1,0:T(8,128)(2,1)} %pack.13), channel_id=1, source_target_pairs={{0,1},{1,0},{2,3},{3,2},{4,5},{5,4},{6,7},{7,6},{8,9},{9,8},{10,11... | collective-permute-start | bytes 2752520 | tf_op jit(solution)/shard_map/ppermute | solution.py:25
  5.4 65.1 %collective-permute-start.39 = (bf16[1792,256]{1,0:T(8,128)(2,1)}, bf16[1792,256]{1,0:T(8,128)(2,1)S(1)}, u32[]{:S(2)}, u32[]{:S(2)}) collective-permute-start(bf16[1792,256]{1,0:T(8,128)(2,1)} %pack.14), channel_id=1, source_target_pairs={{0,2},{1,3},{2,0},{3,1},{4,6},{5,7},{6,4},{7,5},{8,10},{9,11},{10,... | collective-permute-start | bytes 2752520 | tf_op jit(solution)/shard_map/ppermute | solution.py:25
  69.1 53.4 %collective-permute-start.26 = (bf16[1792,256]{1,0:T(8,128)(2,1)}, bf16[1792,256]{1,0:T(8,128)(2,1)}, u32[]{:S(2)}, u32[]{:S(2)}) collective-permute-start(bf16[1792,256]{1,0:T(8,128)(2,1)} %get-tuple-element.98), channel_id=1, source_target_pairs={{0,3},{1,2},{2,1},{3,0},{4,7},{5,6},{6,5},{7,4},{8,11},{9,10},{10,... | collective-permute-start | bytes 2752520 | tf_op jit(solution)/shard_map/ppermute | solution.py:25
  70.5 60.0 %collective-permute-start.14 = (bf16[1792,256]{1,0:T(8,128)(2,1)}, bf16[1792,256]{1,0:T(8,128)(2,1)S(1)}, u32[]{:S(2)}, u32[]{:S(2)}) collective-permute-start(bf16[1792,256]{1,0:T(8,128)(2,1)} %get-tuple-element.85), channel_id=1, source_target_pairs={{0,1},{1,0},{2,3},{3,2},{4,5},{5,4},{6,7},{7,6},{8,9},{9,8},{10,11... | collective-permute-start | bytes 2752520 | tf_op jit(solution)/shard_map/ppermute | solution.py:25
  83.2 88.6 %collective-permute-start.15 = (bf16[1792,256]{1,0:T(8,128)(2,1)}, bf16[1792,256]{1,0:T(8,128)(2,1)S(1)}, u32[]{:S(2)}, u32[]{:S(2)}) collective-permute-start(bf16[1792,256]{1,0:T(8,128)(2,1)} %get-tuple-element.86), channel_id=1, source_target_pairs={{0,2},{1,3},{2,0},{3,1},{4,6},{5,7},{6,4},{7,5},{8,10},{9,11},{10,... | collective-permute-start | bytes 2752520 | tf_op jit(solution)/shard_map/ppermute | solution.py:25
  91.2 80.7 %collective-permute-start.16 = (bf16[1792,256]{1,0:T(8,128)(2,1)}, bf16[1792,256]{1,0:T(8,128)(2,1)S(1)}, u32[]{:S(2)}, u32[]{:S(2)}) collective-permute-start(bf16[1792,256]{1,0:T(8,128)(2,1)} %get-tuple-element.87), channel_id=1, source_target_pairs={{0,3},{1,2},{2,1},{3,0},{4,7},{5,6},{6,5},{7,4},{8,11},{9,10},{10,... | collective-permute-start | bytes 2752520 | tf_op jit(solution)/shard_map/ppermute | solution.py:25
  109.4 63.4 %collective-permute-start = (bf16[1792,256]{1,0:T(8,128)(2,1)}, bf16[1792,256]{1,0:T(8,128)(2,1)S(1)}, u32[]{:S(2)}, u32[]{:S(2)}) collective-permute-start(bf16[1792,256]{1,0:T(8,128)(2,1)} %get-tuple-element.70), channel_id=1, source_target_pairs={{0,1},{1,0},{2,3},{3,2},{4,5},{5,4},{6,7},{7,6},{8,9},{9,8},{10,11... | collective-permute-start | bytes 2752520 | tf_op jit(solution)/shard_map/ppermute | solution.py:25
  122.5 65.4 %collective-permute-start.1 = (bf16[1792,256]{1,0:T(8,128)(2,1)}, bf16[1792,256]{1,0:T(8,128)(2,1)S(1)}, u32[]{:S(2)}, u32[]{:S(2)}) collective-permute-start(bf16[1792,256]{1,0:T(8,128)(2,1)} %get-tuple-element.71), channel_id=1, source_target_pairs={{0,2},{1,3},{2,0},{3,1},{4,6},{5,7},{6,4},{7,5},{8,10},{9,11},{10,... | collective-permute-start | bytes 2752520 | tf_op jit(solution)/shard_map/ppermute | solution.py:25
  130.6 70.5 %collective-permute-start.2 = (bf16[1792,256]{1,0:T(8,128)(2,1)}, bf16[1792,256]{1,0:T(8,128)(2,1)S(1)}, u32[]{:S(2)}, u32[]{:S(2)}) collective-permute-start(bf16[1792,256]{1,0:T(8,128)(2,1)} %get-tuple-element.72), channel_id=1, source_target_pairs={{0,3},{1,2},{2,1},{3,0},{4,7},{5,6},{6,5},{7,4},{8,11},{9,10},{10,... | collective-permute-start | bytes 2752520 | tf_op jit(solution)/shard_map/ppermute | solution.py:25
  171.8 42.0 %collective-permute-start.41 = (bf16[768,256]{1,0:T(8,128)(2,1)S(1)}, bf16[768,256]{1,0:T(8,128)(2,1)S(1)}, u32[]{:S(2)}, u32[]{:S(2)}) collective-permute-start(bf16[768,256]{1,0:T(8,128)(2,1)S(1)} %get-tuple-element.112), channel_id=1, source_target_pairs={{0,1},{1,0},{2,3},{3,2},{4,5},{5,4},{6,7},{7,6},{8,9},{9,8},{10,11... | collective-permute-start | bytes 1179656 | tf_op jit(solution)/shard_map/ppermute | solution.py:25
  172.9 80.0 %collective-permute-start.42 = (bf16[768,256]{1,0:T(8,128)(2,1)S(1)}, bf16[768,256]{1,0:T(8,128)(2,1)S(1)}, u32[]{:S(2)}, u32[]{:S(2)}) collective-permute-start(bf16[768,256]{1,0:T(8,128)(2,1)S(1)} %get-tuple-element.113), channel_id=1, source_target_pairs={{0,4},{1,5},{2,6},{3,7},{4,8},{5,9},{6,10},{7,11},{8,12},{9,13},{1... | collective-permute-start | bytes 1179656 | tf_op jit(solution)/shard_map/ppermute | solution.py:25
  172.9 80.0 %collective-permute-start.43 = (bf16[768,256]{1,0:T(8,128)(2,1)S(1)}, bf16[768,256]{1,0:T(8,128)(2,1)S(1)}, u32[]{:S(2)}, u32[]{:S(2)}) collective-permute-start(bf16[768,256]{1,0:T(8,128)(2,1)S(1)} %get-tuple-element.114), channel_id=1, source_target_pairs={{0,5},{1,4},{2,7},{3,6},{4,9},{5,8},{6,11},{7,10},{8,13},{9,12},{1... | collective-permute-start | bytes 1179656 | tf_op jit(solution)/shard_map/ppermute | solution.py:25
  188.0 65.5 %collective-permute-start.44 = (bf16[768,256]{1,0:T(8,128)(2,1)S(1)}, bf16[768,256]{1,0:T(8,128)(2,1)S(1)}, u32[]{:S(2)}, u32[]{:S(2)}) collective-permute-start(bf16[768,256]{1,0:T(8,128)(2,1)S(1)} %get-tuple-element.115), channel_id=1, source_target_pairs={{0,6},{1,7},{2,4},{3,5},{4,10},{5,11},{6,8},{7,9},{8,14},{9,15},{1... | collective-permute-start | bytes 1179656 | tf_op jit(solution)/shard_map/ppermute | solution.py:25
  202.0 51.5 %collective-permute-start.45 = (bf16[768,256]{1,0:T(8,128)(2,1)S(1)}, bf16[768,256]{1,0:T(8,128)(2,1)S(1)}, u32[]{:S(2)}, u32[]{:S(2)}) collective-permute-start(bf16[768,256]{1,0:T(8,128)(2,1)S(1)} %get-tuple-element.116), channel_id=1, source_target_pairs={{0,7},{1,6},{2,5},{3,4},{4,11},{5,10},{6,9},{7,8},{8,15},{9,14},{1... | collective-permute-start | bytes 1179656 | tf_op jit(solution)/shard_map/ppermute | solution.py:25
  252.9 41.3 %collective-permute-start.31 = (bf16[768,256]{1,0:T(8,128)(2,1)S(1)}, bf16[768,256]{1,0:T(8,128)(2,1)S(1)}, u32[]{:S(2)}, u32[]{:S(2)}) collective-permute-start(bf16[768,256]{1,0:T(8,128)(2,1)S(1)} %get-tuple-element.104), channel_id=1, source_target_pairs={{0,1},{1,0},{2,3},{3,2},{4,5},{5,4},{6,7},{7,6},{8,9},{9,8},{10,11... | collective-permute-start | bytes 1179656 | tf_op jit(solution)/shard_map/ppermute | solution.py:25
  253.5 41.9 %collective-permute-start.32 = (bf16[768,256]{1,0:T(8,128)(2,1)S(1)}, bf16[768,256]{1,0:T(8,128)(2,1)S(1)}, u32[]{:S(2)}, u32[]{:S(2)}) collective-permute-start(bf16[768,256]{1,0:T(8,128)(2,1)S(1)} %get-tuple-element.105), channel_id=1, source_target_pairs={{0,4},{1,5},{2,6},{3,7},{4,8},{5,9},{6,10},{7,11},{8,12},{9,13},{1... | collective-permute-start | bytes 1179656 | tf_op jit(solution)/shard_map/ppermute | solution.py:25
  253.5 42.1 %collective-permute-start.33 = (bf16[768,256]{1,0:T(8,128)(2,1)S(1)}, bf16[768,256]{1,0:T(8,128)(2,1)S(1)}, u32[]{:S(2)}, u32[]{:S(2)}) collective-permute-start(bf16[768,256]{1,0:T(8,128)(2,1)S(1)} %get-tuple-element.106), channel_id=1, source_target_pairs={{0,5},{1,4},{2,7},{3,6},{4,9},{5,8},{6,11},{7,10},{8,13},{9,12},{1... | collective-permute-start | bytes 1179656 | tf_op jit(solution)/shard_map/ppermute | solution.py:25
  253.6 42.8 %collective-permute-start.34 = (bf16[768,256]{1,0:T(8,128)(2,1)S(1)}, bf16[768,256]{1,0:T(8,128)(2,1)S(1)}, u32[]{:S(2)}, u32[]{:S(2)}) collective-permute-start(bf16[768,256]{1,0:T(8,128)(2,1)S(1)} %get-tuple-element.107), channel_id=1, source_target_pairs={{0,6},{1,7},{2,4},{3,5},{4,10},{5,11},{6,8},{7,9},{8,14},{9,15},{1... | collective-permute-start | bytes 1179656 | tf_op jit(solution)/shard_map/ppermute | solution.py:25
  310.7 59.6 %collective-permute-start.19 = (bf16[768,256]{1,0:T(8,128)(2,1)S(1)}, bf16[768,256]{1,0:T(8,128)(2,1)S(1)}, u32[]{:S(2)}, u32[]{:S(2)}) collective-permute-start(bf16[768,256]{1,0:T(8,128)(2,1)S(1)} %get-tuple-element.91), channel_id=1, source_target_pairs={{0,5},{1,4},{2,7},{3,6},{4,9},{5,8},{6,11},{7,10},{8,13},{9,12},{1... | collective-permute-start | bytes 1179656 | tf_op jit(solution)/shard_map/ppermute | solution.py:25
  313.9 56.4 %collective-permute-start.20 = (bf16[768,256]{1,0:T(8,128)(2,1)S(1)}, bf16[768,256]{1,0:T(8,128)(2,1)S(1)}, u32[]{:S(2)}, u32[]{:S(2)}) collective-permute-start(bf16[768,256]{1,0:T(8,128)(2,1)S(1)} %get-tuple-element.92), channel_id=1, source_target_pairs={{0,6},{1,7},{2,4},{3,5},{4,10},{5,11},{6,8},{7,9},{8,14},{9,15},{1... | collective-permute-start | bytes 1179656 | tf_op jit(solution)/shard_map/ppermute | solution.py:25
  321.0 56.7 %collective-permute-start.21 = (bf16[768,256]{1,0:T(8,128)(2,1)S(1)}, bf16[768,256]{1,0:T(8,128)(2,1)S(1)}, u32[]{:S(2)}, u32[]{:S(2)}) collective-permute-start(bf16[768,256]{1,0:T(8,128)(2,1)S(1)} %get-tuple-element.93), channel_id=1, source_target_pairs={{0,7},{1,6},{2,5},{3,4},{4,11},{5,10},{6,9},{7,8},{8,15},{9,14},{1... | collective-permute-start | bytes 1179656 | tf_op jit(solution)/shard_map/ppermute | solution.py:25
  326.7 51.1 %collective-permute-start.22 = (bf16[768,256]{1,0:T(8,128)(2,1)S(1)}, bf16[768,256]{1,0:T(8,128)(2,1)S(1)}, u32[]{:S(2)}, u32[]{:S(2)}) collective-permute-start(bf16[768,256]{1,0:T(8,128)(2,1)S(1)} %get-tuple-element.94), channel_id=1, source_target_pairs={{0,2},{1,3},{2,0},{3,1},{4,6},{5,7},{6,4},{7,5},{8,10},{9,11},{10,... | collective-permute-start | bytes 1179656 | tf_op jit(solution)/shard_map/ppermute | solution.py:25
  327.4 51.8 %collective-permute-start.23 = (bf16[768,256]{1,0:T(8,128)(2,1)S(1)}, bf16[768,256]{1,0:T(8,128)(2,1)S(1)}, u32[]{:S(2)}, u32[]{:S(2)}) collective-permute-start(bf16[768,256]{1,0:T(8,128)(2,1)S(1)} %get-tuple-element.95), channel_id=1, source_target_pairs={{0,3},{1,2},{2,1},{3,0},{4,7},{5,6},{6,5},{7,4},{8,11},{9,10},{10,... | collective-permute-start | bytes 1179656 | tf_op jit(solution)/shard_map/ppermute | solution.py:25
  377.8 40.8 %collective-permute-start.9 = (bf16[768,256]{1,0:T(8,128)(2,1)S(1)}, bf16[768,256]{1,0:T(8,128)(2,1)S(1)}, u32[]{:S(2)}, u32[]{:S(2)}) collective-permute-start(bf16[768,256]{1,0:T(8,128)(2,1)S(1)} %get-tuple-element.79), channel_id=1, source_target_pairs={{0,6},{1,7},{2,4},{3,5},{4,10},{5,11},{6,8},{7,9},{8,14},{9,15},{1... | collective-permute-start | bytes 1179656 | tf_op jit(solution)/shard_map/ppermute | solution.py:25
  (73 other events, 2536.0 us)

commit v2 on v1

--- a/solution.py
+++ b/solution.py
@@ -64,6 +64,56 @@
         cost_estimate=cost(0, 4 * sum(sizes) * width * len(peers)),
     )(me, *[a for _ in peers for a, _ in arrays])
     return dict(zip(peers, out))
+
+
+def packed_by_copies(arrays, me, sample, first, units, heads_each, peers):
+    (peer,) = peers
+    rows, model_width = arrays[0][0].shape[2], arrays[0][0].shape[4]
+    width = units * HDIM
+    share, offset = heads_each // units, first // units
+    parts = COLS // HALF
+    total = sum(rows * (parts if half is None else 1) for _, half in arrays)
+
+    def kernel(me_ref, *refs):
+        out, sems = refs[-2:]
+        head = pl.multiple_of(((me_ref[0] ^ peer) * share + offset) * width, width)
+        copies, at = [], 0
+        for i, (_, half) in enumerate(arrays):
+            size = rows * (parts if half is None else 1)
+            lanes = pl.ds(head, width)
+            if half is None:
+                piece = refs[i].at[sample, :, :, lanes]
+            else:
+                piece = refs[i].at[sample, :, half, :, lanes]
+            copies.append(pltpu.make_async_copy(piece, out.at[pl.ds(at, size)], sems.at[i]))
+            at += size
+        for copy in copies:
+            copy.start()
+        for copy in copies:
+            copy.wait()
+
+    samples = arrays[0][0].shape[0]
+    views = [
+        a.reshape((samples, rows * parts, HALF, model_width) if half is None
+                  else (samples, rows, parts, HALF, model_width))
+        for a, half in arrays
+    ]
+    anywhere = pl.BlockSpec(memory_space=pl.ANY)
+    out = pl.pallas_call(
+        kernel,
+        grid_spec=pltpu.PrefetchScalarGridSpec(
+            num_scalar_prefetch=1,
+            grid=(1,),
+            in_specs=[anywhere] * len(views),
+            out_specs=anywhere,
+            scratch_shapes=[pltpu.SemaphoreType.DMA((len(views),))],
+        ),
+        out_shape=jax.ShapeDtypeStruct((total, HALF, width), jnp.bfloat16),
+        compiler_params=pltpu.CompilerParams(vmem_limit_bytes=2**20),
+        name="pack",
+        cost_estimate=cost(0, 4 * total * HALF * width),
+    )(me, *views)
+    return {peer: out.reshape(total * HALF, width)}
 
 
 def window_grads(args, me, sample, first, units, heads_each, seqs, arrived, arrived_west):
@@ -235,7 +285,8 @@
     def sent(arrays, place, peers, west):
         nonlocal step
         step += 1
-        blocks = packed(arrays, me, *place, peers)
+        pack = packed_by_copies if step == 1 else packed
+        blocks = pack(arrays, me, *place, peers)
         return {k: exchanged(blocks[k], k, west) for k in peers}
 
     for sample, first in chunks:

time: 422 us -> 430 us (1.019)
  starting transfers between devices: 84.9 us -> 71.9 us
  waiting for transfers between devices: 137 us -> 150 us
  local copies, waits for them, and re-layouts: 14.5 us -> 23.9 us
    ppermute x48, starting transfers between devices: 84.9 us -> 71.9 us  [exchanged(): return lax.ppermute(block, ('win', 'seq'), route)]
    ppermute x48, waiting for transfers between devices: 137 us -> 150 us  [exchanged(): return lax.ppermute(block, ('win', 'seq'), route)]
    unnamed x98 -> x108, local copies, waits for them, and re-layouts: 14.5 us -> 23.9 us
    pallas_call x8 -> x7, Pallas kernels: 21 us -> 18.9 us  [packed(): pl.pallas_call(kernel, grid_spec=pltpu.PrefetchScalarGridSpec(num_scalar_...]
  transfers between devices with their start and end apart: 48 -> 48, of which waited for: 15 -> 14; matrix products, arithmetic and copies ran while one was open for 0% -> 0% of each run, Pallas kernels for 43% -> 42%
where the time goes in v2:
time: 430 us; the launch traced here: 428 us
  Pallas kernels  181 us (42%)
  waiting for transfers between devices  150 us (35%)
  starting transfers between devices  71.9 us (17%)
  local copies, waits for them, and re-layouts  23.9 us (6%)
    ppermute x48, waiting for transfers between devices, exchanged(): return lax.ppermute(block, ('win', 'seq'), route)  150 us
    pallas_call x4, Pallas kernels, window_grads(): pl.pallas_call(kernel, grid_spec=pltpu.PrefetchScalarGridSpec(num_scalar_...  147 us
    ppermute x48, starting transfers between devices, exchanged(): return lax.ppermute(block, ('win', 'seq'), route)  71.9 us
    unnamed x108, local copies, waits for them, and re-layouts  23.9 us
    pallas_call x7, Pallas kernels, packed(): pl.pallas_call(kernel, grid_spec=pltpu.PrefetchScalarGridSpec(num_scalar_...  18.9 us
    pallas_call x6, Pallas kernels, placed(): pl.pallas_call(kernel, grid_spec=pltpu.PrefetchScalarGridSpec(num_scalar_...  15.5 us
  transfers between devices with their start and end apart: 48, of which 14 were waited for; matrix products, arithmetic and copies ran while one was open for 0% of the time, Pallas kernels for 42%

profile of v2, /device:TPU:0, one launch (start us, length us, event | category | flops | bytes accessed | tf_op | source)
XLA Modules:
  0.0 428.0 jit_solution(3108784864328676017)
XLA Ops:
  10.2 4.6 %collective-permute-start.27 = (bf16[256,512]{1,0:T(8,128)(2,1)}, bf16[256,512]{1,0:T(8,128)(2,1)S(1)}, u32[]{:S(2)}, u32[]{:S(2)}) collective-permute-start(bf16[256,512]{1,0:T(8,128)(2,1)} %get-tuple-element.99), channel_id=1, source_target_pairs={{0,28},{1,29},{2,30},{3,31},{4,0},{5,1},{6,2},{7,3},{8,4},{9,5},{1... | collective-permute-start | bytes 786440 | tf_op jit(solution)/shard_map/ppermute | solution.py:25
  18.2 3.6 collective-permute-done.27.refs_3_
  30.6 6.1 %collective-permute-done.29.refs_5_ = bf16[256,512]{1,0:T(8,128)(2,1)S(1)} collective-permute-done((bf16[256,512]{1,0:T(8,128)(2,1)}, bf16[256,512]{1,0:T(8,128)(2,1)S(1)}, u32[]{:S(2)}, u32[]{:S(2)}) %collective-permute-start.29) | collective-permute-done | bytes 262176 | tf_op jit(solution)/shard_map/ppermute | solution.py:25
  44.8 8.0 %collective-permute-done.3.refs_3_ = bf16[256,512]{1,0:T(8,128)(2,1)S(1)} collective-permute-done((bf16[256,512]{1,0:T(8,128)(2,1)}, bf16[256,512]{1,0:T(8,128)(2,1)S(1)}, u32[]{:S(2)}, u32[]{:S(2)}) %collective-permute-start.3) | collective-permute-done | bytes 262176 | tf_op jit(solution)/shard_map/ppermute | solution.py:25
  52.8 3.5 pack.11
  68.6 6.4 %collective-permute-start.39 = (bf16[1792,256]{1,0:T(8,128)(2,1)S(1)}, bf16[1792,256]{1,0:T(8,128)(2,1)}, u32[]{:S(2)}, u32[]{:S(2)}) collective-permute-start(bf16[1792,256]{1,0:T(8,128)(2,1)S(1)} %bitcast.123), channel_id=1, source_target_pairs={{0,2},{1,3},{2,0},{3,1},{4,6},{5,7},{6,4},{7,5},{8,10},{9,11},{10,... | collective-permute-start | bytes 2752520 | tf_op jit(solution)/shard_map/ppermute | solution.py:25
  81.3 15.1 %collective-permute-done.39.refs_1_ = bf16[1792,256]{1,0:T(8,128)(2,1)} collective-permute-done((bf16[1792,256]{1,0:T(8,128)(2,1)S(1)}, bf16[1792,256]{1,0:T(8,128)(2,1)}, u32[]{:S(2)}, u32[]{:S(2)}) %collective-permute-start.39) | collective-permute-done | bytes 917536 | tf_op jit(solution)/shard_map/ppermute | solution.py:25
  98.4 17.6 %collective-permute-done.25.refs_1_ = bf16[1792,256]{1,0:T(8,128)(2,1)} collective-permute-done((bf16[1792,256]{1,0:T(8,128)(2,1)}, bf16[1792,256]{1,0:T(8,128)(2,1)}, u32[]{:S(2)}, u32[]{:S(2)}) %collective-permute-start.25) | collective-permute-done | bytes 917536 | tf_op jit(solution)/shard_map/ppermute | solution.py:25
  116.0 19.2 %collective-permute-done.26.refs_2_ = bf16[1792,256]{1,0:T(8,128)(2,1)} collective-permute-done((bf16[1792,256]{1,0:T(8,128)(2,1)}, bf16[1792,256]{1,0:T(8,128)(2,1)}, u32[]{:S(2)}, u32[]{:S(2)}) %collective-permute-start.26) | collective-permute-done | bytes 917536 | tf_op jit(solution)/shard_map/ppermute | solution.py:25
  140.9 36.7 %grads.7 = (bf16[768,256]{1,0:T(8,128)(2,1)S(1)}, bf16[768,256]{1,0:T(8,128)(2,1)S(1)}, bf16[768,256]{1,0:T(8,128)(2,1)S(1)}, bf16[768,256]{1,0:T(8,128)(2,1)S(1...) custom-call(s32[1]{0:T(128)} %bitcast.me_ref, ...), custom_call_target="tpu_custom_call" | custom-call | flops 10737418240 | bytes 7340032 | tf_op jit(solution)/shard_map/grads/pallas_call | solution.py:205
  179.6 15.0 %collective-permute-done.1.refs_1_ = bf16[1792,256]{1,0:T(8,128)(2,1)S(1)} collective-permute-done((bf16[1792,256]{1,0:T(8,128)(2,1)}, bf16[1792,256]{1,0:T(8,128)(2,1)S(1)}, u32[]{:S(2)}, u32[]{:S(2)}) %collective-permute-start.1) | collective-permute-done | bytes 917536 | tf_op jit(solution)/shard_map/ppermute | solution.py:25
  194.5 16.9 %collective-permute-done.2.refs_2_ = bf16[1792,256]{1,0:T(8,128)(2,1)S(1)} collective-permute-done((bf16[1792,256]{1,0:T(8,128)(2,1)}, bf16[1792,256]{1,0:T(8,128)(2,1)S(1)}, u32[]{:S(2)}, u32[]{:S(2)}) %collective-permute-start.2) | collective-permute-done | bytes 917536 | tf_op jit(solution)/shard_map/ppermute | solution.py:25
  211.5 7.1 %collective-permute-start.45 = (bf16[768,256]{1,0:T(8,128)(2,1)S(1)}, bf16[768,256]{1,0:T(8,128)(2,1)S(1)}, u32[]{:S(2)}, u32[]{:S(2)}) collective-permute-start(bf16[768,256]{1,0:T(8,128)(2,1)S(1)} %get-tuple-element.116), channel_id=1, source_target_pairs={{0,7},{1,6},{2,5},{3,4},{4,11},{5,10},{6,9},{7,8},{8,15},{9,14},{1... | collective-permute-start | bytes 1179656 | tf_op jit(solution)/shard_map/ppermute | solution.py:25
  221.1 36.8 %grads.6 = (bf16[768,256]{1,0:T(8,128)(2,1)S(1)}, bf16[768,256]{1,0:T(8,128)(2,1)S(1)}, bf16[768,256]{1,0:T(8,128)(2,1)S(1)}, bf16[768,256]{1,0:T(8,128)(2,1)S(1...) custom-call(s32[1]{0:T(128)} %bitcast.me_ref, ...), custom_call_target="tpu_custom_call" | custom-call | flops 10737418240 | bytes 7340032 | tf_op jit(solution)/shard_map/grads/pallas_call | solution.py:205
  261.3 36.5 %grads.5 = (bf16[768,256]{1,0:T(8,128)(2,1)S(1)}, bf16[768,256]{1,0:T(8,128)(2,1)S(1)}, bf16[768,256]{1,0:T(8,128)(2,1)S(1)}, bf16[768,256]{1,0:T(8,128)(2,1)S(1...) custom-call(s32[1]{0:T(128)} %bitcast.me_ref, ...), custom_call_target="tpu_custom_call" | custom-call | flops 10737418240 | bytes 7340032 | tf_op jit(solution)/shard_map/grads/pallas_call | solution.py:205
  301.1 17.2 %collective-permute-done.35 = bf16[768,256]{1,0:T(8,128)(2,1)S(1)} collective-permute-done((bf16[768,256]{1,0:T(8,128)(2,1)S(1)}, bf16[768,256]{1,0:T(8,128)(2,1)S(1)}, u32[]{:S(2)}, u32[]{:S(2)}) %collective-permute-start.35) | collective-permute-done | bytes 393248 | tf_op jit(solution)/shard_map/ppermute | solution.py:25
  318.7 5.2 %collective-permute-start.20 = (bf16[768,256]{1,0:T(8,128)(2,1)S(1)}, bf16[768,256]{1,0:T(8,128)(2,1)S(1)}, u32[]{:S(2)}, u32[]{:S(2)}) collective-permute-start(bf16[768,256]{1,0:T(8,128)(2,1)S(1)} %get-tuple-element.92), channel_id=1, source_target_pairs={{0,6},{1,7},{2,4},{3,5},{4,10},{5,11},{6,8},{7,9},{8,14},{9,15},{1... | collective-permute-start | bytes 1179656 | tf_op jit(solution)/shard_map/ppermute | solution.py:25
  326.1 7.9 %collective-permute-start.21 = (bf16[768,256]{1,0:T(8,128)(2,1)S(1)}, bf16[768,256]{1,0:T(8,128)(2,1)S(1)}, u32[]{:S(2)}, u32[]{:S(2)}) collective-permute-start(bf16[768,256]{1,0:T(8,128)(2,1)S(1)} %get-tuple-element.93), channel_id=1, source_target_pairs={{0,7},{1,6},{2,5},{3,4},{4,11},{5,10},{6,9},{7,8},{8,15},{9,14},{1... | collective-permute-start | bytes 1179656 | tf_op jit(solution)/shard_map/ppermute | solution.py:25
  340.2 36.5 %grads.4 = (bf16[768,256]{1,0:T(8,128)(2,1)S(1)}, bf16[768,256]{1,0:T(8,128)(2,1)S(1)}, bf16[768,256]{1,0:T(8,128)(2,1)S(1)}, bf16[768,256]{1,0:T(8,128)(2,1)S(1...) custom-call(s32[1]{0:T(128)} %bitcast.me_ref, ...), custom_call_target="tpu_custom_call" | custom-call | flops 10737418240 | bytes 7340032 | tf_op jit(solution)/shard_map/grads/pallas_call | solution.py:205
  377.5 7.6 %collective-permute-start.12 = (bf16[768,256]{1,0:T(8,128)(2,1)S(1)}, bf16[768,256]{1,0:T(8,128)(2,1)S(1)}, u32[]{:S(2)}, u32[]{:S(2)}) collective-permute-start(bf16[768,256]{1,0:T(8,128)(2,1)S(1)} %get-tuple-element.83), channel_id=1, source_target_pairs={{0,4},{1,5},{2,6},{3,7},{4,8},{5,9},{6,10},{7,11},{8,12},{9,13},{1... | collective-permute-start | bytes 1179656 | tf_op jit(solution)/shard_map/ppermute | solution.py:25
  389.1 22.4 %collective-permute-done.12 = bf16[768,256]{1,0:T(8,128)(2,1)S(1)} collective-permute-done((bf16[768,256]{1,0:T(8,128)(2,1)S(1)}, bf16[768,256]{1,0:T(8,128)(2,1)S(1)}, u32[]{:S(2)}, u32[]{:S(2)}) %collective-permute-start.12) | collective-permute-done | bytes 393248 | tf_op jit(solution)/shard_map/ppermute | solution.py:25
  412.2 3.7 place.6
  415.9 3.7 place.7
  419.6 3.7 place.8
  (198 shorter events, 85.7 us)
Async XLA Ops:
  2.8 73.1 %collective-permute-start.38 = (bf16[1792,256]{1,0:T(8,128)(2,1)}, bf16[1792,256]{1,0:T(8,128)(2,1)S(1)}, u32[]{:S(2)}, u32[]{:S(2)}) collective-permute-start(bf16[1792,256]{1,0:T(8,128)(2,1)} %pack.13), channel_id=1, source_target_pairs={{0,1},{1,0},{2,3},{3,2},{4,5},{5,4},{6,7},{7,6},{8,9},{9,8},{10,11... | collective-permute-start | bytes 2752520 | tf_op jit(solution)/shard_map/ppermute | solution.py:25
  5.4 72.2 %collective-permute-start.40 = (bf16[1792,256]{1,0:T(8,128)(2,1)}, bf16[1792,256]{1,0:T(8,128)(2,1)}, u32[]{:S(2)}, u32[]{:S(2)}) collective-permute-start(bf16[1792,256]{1,0:T(8,128)(2,1)} %pack.15), channel_id=1, source_target_pairs={{0,3},{1,2},{2,1},{3,0},{4,7},{5,6},{6,5},{7,4},{8,11},{9,10},{10,... | collective-permute-start | bytes 2752520 | tf_op jit(solution)/shard_map/ppermute | solution.py:25
  75.8 40.2 %collective-permute-start.25 = (bf16[1792,256]{1,0:T(8,128)(2,1)}, bf16[1792,256]{1,0:T(8,128)(2,1)}, u32[]{:S(2)}, u32[]{:S(2)}) collective-permute-start(bf16[1792,256]{1,0:T(8,128)(2,1)} %get-tuple-element.97), channel_id=1, source_target_pairs={{0,2},{1,3},{2,0},{3,1},{4,6},{5,7},{6,4},{7,5},{8,10},{9,11},{10,... | collective-permute-start | bytes 2752520 | tf_op jit(solution)/shard_map/ppermute | solution.py:25
  75.8 59.3 %collective-permute-start.26 = (bf16[1792,256]{1,0:T(8,128)(2,1)}, bf16[1792,256]{1,0:T(8,128)(2,1)}, u32[]{:S(2)}, u32[]{:S(2)}) collective-permute-start(bf16[1792,256]{1,0:T(8,128)(2,1)} %get-tuple-element.98), channel_id=1, source_target_pairs={{0,3},{1,2},{2,1},{3,0},{4,7},{5,6},{6,5},{7,4},{8,11},{9,10},{10,... | collective-permute-start | bytes 2752520 | tf_op jit(solution)/shard_map/ppermute | solution.py:25
  77.6 57.6 %collective-permute-start.14 = (bf16[1792,256]{1,0:T(8,128)(2,1)}, bf16[1792,256]{1,0:T(8,128)(2,1)S(1)}, u32[]{:S(2)}, u32[]{:S(2)}) collective-permute-start(bf16[1792,256]{1,0:T(8,128)(2,1)} %get-tuple-element.85), channel_id=1, source_target_pairs={{0,1},{1,0},{2,3},{3,2},{4,5},{5,4},{6,7},{7,6},{8,9},{9,8},{10,11... | collective-permute-start | bytes 2752520 | tf_op jit(solution)/shard_map/ppermute | solution.py:25
  96.3 82.1 %collective-permute-start.15 = (bf16[1792,256]{1,0:T(8,128)(2,1)}, bf16[1792,256]{1,0:T(8,128)(2,1)S(1)}, u32[]{:S(2)}, u32[]{:S(2)}) collective-permute-start(bf16[1792,256]{1,0:T(8,128)(2,1)} %get-tuple-element.86), channel_id=1, source_target_pairs={{0,2},{1,3},{2,0},{3,1},{4,6},{5,7},{6,4},{7,5},{8,10},{9,11},{10,... | collective-permute-start | bytes 2752520 | tf_op jit(solution)/shard_map/ppermute | solution.py:25
  98.4 80.3 %collective-permute-start.16 = (bf16[1792,256]{1,0:T(8,128)(2,1)}, bf16[1792,256]{1,0:T(8,128)(2,1)S(1)}, u32[]{:S(2)}, u32[]{:S(2)}) collective-permute-start(bf16[1792,256]{1,0:T(8,128)(2,1)} %get-tuple-element.87), channel_id=1, source_target_pairs={{0,3},{1,2},{2,1},{3,0},{4,7},{5,6},{6,5},{7,4},{8,11},{9,10},{10,... | collective-permute-start | bytes 2752520 | tf_op jit(solution)/shard_map/ppermute | solution.py:25
  116.0 62.6 %collective-permute-start = (bf16[1792,256]{1,0:T(8,128)(2,1)}, bf16[1792,256]{1,0:T(8,128)(2,1)S(1)}, u32[]{:S(2)}, u32[]{:S(2)}) collective-permute-start(bf16[1792,256]{1,0:T(8,128)(2,1)} %get-tuple-element.70), channel_id=1, source_target_pairs={{0,1},{1,0},{2,3},{3,2},{4,5},{5,4},{6,7},{7,6},{8,9},{9,8},{10,11... | collective-permute-start | bytes 2752520 | tf_op jit(solution)/shard_map/ppermute | solution.py:25
  135.2 59.3 %collective-permute-start.1 = (bf16[1792,256]{1,0:T(8,128)(2,1)}, bf16[1792,256]{1,0:T(8,128)(2,1)S(1)}, u32[]{:S(2)}, u32[]{:S(2)}) collective-permute-start(bf16[1792,256]{1,0:T(8,128)(2,1)} %get-tuple-element.71), channel_id=1, source_target_pairs={{0,2},{1,3},{2,0},{3,1},{4,6},{5,7},{6,4},{7,5},{8,10},{9,11},{10,... | collective-permute-start | bytes 2752520 | tf_op jit(solution)/shard_map/ppermute | solution.py:25
  135.2 76.3 %collective-permute-start.2 = (bf16[1792,256]{1,0:T(8,128)(2,1)}, bf16[1792,256]{1,0:T(8,128)(2,1)S(1)}, u32[]{:S(2)}, u32[]{:S(2)}) collective-permute-start(bf16[1792,256]{1,0:T(8,128)(2,1)} %get-tuple-element.72), channel_id=1, source_target_pairs={{0,3},{1,2},{2,1},{3,0},{4,7},{5,6},{6,5},{7,4},{8,11},{9,10},{10,... | collective-permute-start | bytes 2752520 | tf_op jit(solution)/shard_map/ppermute | solution.py:25
  178.4 40.2 %collective-permute-start.41 = (bf16[768,256]{1,0:T(8,128)(2,1)S(1)}, bf16[768,256]{1,0:T(8,128)(2,1)S(1)}, u32[]{:S(2)}, u32[]{:S(2)}) collective-permute-start(bf16[768,256]{1,0:T(8,128)(2,1)S(1)} %get-tuple-element.112), channel_id=1, source_target_pairs={{0,1},{1,0},{2,3},{3,2},{4,5},{5,4},{6,7},{7,6},{8,9},{9,8},{10,11... | collective-permute-start | bytes 1179656 | tf_op jit(solution)/shard_map/ppermute | solution.py:25
  178.6 80.0 %collective-permute-start.42 = (bf16[768,256]{1,0:T(8,128)(2,1)S(1)}, bf16[768,256]{1,0:T(8,128)(2,1)S(1)}, u32[]{:S(2)}, u32[]{:S(2)}) collective-permute-start(bf16[768,256]{1,0:T(8,128)(2,1)S(1)} %get-tuple-element.113), channel_id=1, source_target_pairs={{0,4},{1,5},{2,6},{3,7},{4,8},{5,9},{6,10},{7,11},{8,12},{9,13},{1... | collective-permute-start | bytes 1179656 | tf_op jit(solution)/shard_map/ppermute | solution.py:25
  179.6 79.2 %collective-permute-start.43 = (bf16[768,256]{1,0:T(8,128)(2,1)S(1)}, bf16[768,256]{1,0:T(8,128)(2,1)S(1)}, u32[]{:S(2)}, u32[]{:S(2)}) collective-permute-start(bf16[768,256]{1,0:T(8,128)(2,1)S(1)} %get-tuple-element.114), channel_id=1, source_target_pairs={{0,5},{1,4},{2,7},{3,6},{4,9},{5,8},{6,11},{7,10},{8,13},{9,12},{1... | collective-permute-start | bytes 1179656 | tf_op jit(solution)/shard_map/ppermute | solution.py:25
  194.5 64.3 %collective-permute-start.44 = (bf16[768,256]{1,0:T(8,128)(2,1)S(1)}, bf16[768,256]{1,0:T(8,128)(2,1)S(1)}, u32[]{:S(2)}, u32[]{:S(2)}) collective-permute-start(bf16[768,256]{1,0:T(8,128)(2,1)S(1)} %get-tuple-element.115), channel_id=1, source_target_pairs={{0,6},{1,7},{2,4},{3,5},{4,10},{5,11},{6,8},{7,9},{8,14},{9,15},{1... | collective-permute-start | bytes 1179656 | tf_op jit(solution)/shard_map/ppermute | solution.py:25
  211.5 49.0 %collective-permute-start.45 = (bf16[768,256]{1,0:T(8,128)(2,1)S(1)}, bf16[768,256]{1,0:T(8,128)(2,1)S(1)}, u32[]{:S(2)}, u32[]{:S(2)}) collective-permute-start(bf16[768,256]{1,0:T(8,128)(2,1)S(1)} %get-tuple-element.116), channel_id=1, source_target_pairs={{0,7},{1,6},{2,5},{3,4},{4,11},{5,10},{6,9},{7,8},{8,15},{9,14},{1... | collective-permute-start | bytes 1179656 | tf_op jit(solution)/shard_map/ppermute | solution.py:25
  218.6 41.9 %collective-permute-start.46 = (bf16[768,256]{1,0:T(8,128)(2,1)S(1)}, bf16[768,256]{1,0:T(8,128)(2,1)S(1)}, u32[]{:S(2)}, u32[]{:S(2)}) collective-permute-start(bf16[768,256]{1,0:T(8,128)(2,1)S(1)} %get-tuple-element.117), channel_id=1, source_target_pairs={{0,2},{1,3},{2,0},{3,1},{4,6},{5,7},{6,4},{7,5},{8,10},{9,11},{10,... | collective-permute-start | bytes 1179656 | tf_op jit(solution)/shard_map/ppermute | solution.py:25
  258.6 40.1 %collective-permute-start.47 = (bf16[768,256]{1,0:T(8,128)(2,1)S(1)}, bf16[768,256]{1,0:T(8,128)(2,1)S(1)}, u32[]{:S(2)}, u32[]{:S(2)}) collective-permute-start(bf16[768,256]{1,0:T(8,128)(2,1)S(1)} %get-tuple-element.118), channel_id=1, source_target_pairs={{0,3},{1,2},{2,1},{3,0},{4,7},{5,6},{6,5},{7,4},{8,11},{9,10},{10,... | collective-permute-start | bytes 1179656 | tf_op jit(solution)/shard_map/ppermute | solution.py:25
  258.7 40.0 %collective-permute-start.31 = (bf16[768,256]{1,0:T(8,128)(2,1)S(1)}, bf16[768,256]{1,0:T(8,128)(2,1)S(1)}, u32[]{:S(2)}, u32[]{:S(2)}) collective-permute-start(bf16[768,256]{1,0:T(8,128)(2,1)S(1)} %get-tuple-element.104), channel_id=1, source_target_pairs={{0,1},{1,0},{2,3},{3,2},{4,5},{5,4},{6,7},{7,6},{8,9},{9,8},{10,11... | collective-permute-start | bytes 1179656 | tf_op jit(solution)/shard_map/ppermute | solution.py:25
  258.9 41.5 %collective-permute-start.32 = (bf16[768,256]{1,0:T(8,128)(2,1)S(1)}, bf16[768,256]{1,0:T(8,128)(2,1)S(1)}, u32[]{:S(2)}, u32[]{:S(2)}) collective-permute-start(bf16[768,256]{1,0:T(8,128)(2,1)S(1)} %get-tuple-element.105), channel_id=1, source_target_pairs={{0,4},{1,5},{2,6},{3,7},{4,8},{5,9},{6,10},{7,11},{8,12},{9,13},{1... | collective-permute-start | bytes 1179656 | tf_op jit(solution)/shard_map/ppermute | solution.py:25
  318.3 59.1 %collective-permute-start.19 = (bf16[768,256]{1,0:T(8,128)(2,1)S(1)}, bf16[768,256]{1,0:T(8,128)(2,1)S(1)}, u32[]{:S(2)}, u32[]{:S(2)}) collective-permute-start(bf16[768,256]{1,0:T(8,128)(2,1)S(1)} %get-tuple-element.91), channel_id=1, source_target_pairs={{0,5},{1,4},{2,7},{3,6},{4,9},{5,8},{6,11},{7,10},{8,13},{9,12},{1... | collective-permute-start | bytes 1179656 | tf_op jit(solution)/shard_map/ppermute | solution.py:25
  318.7 58.8 %collective-permute-start.20 = (bf16[768,256]{1,0:T(8,128)(2,1)S(1)}, bf16[768,256]{1,0:T(8,128)(2,1)S(1)}, u32[]{:S(2)}, u32[]{:S(2)}) collective-permute-start(bf16[768,256]{1,0:T(8,128)(2,1)S(1)} %get-tuple-element.92), channel_id=1, source_target_pairs={{0,6},{1,7},{2,4},{3,5},{4,10},{5,11},{6,8},{7,9},{8,14},{9,15},{1... | collective-permute-start | bytes 1179656 | tf_op jit(solution)/shard_map/ppermute | solution.py:25
  326.1 59.1 %collective-permute-start.21 = (bf16[768,256]{1,0:T(8,128)(2,1)S(1)}, bf16[768,256]{1,0:T(8,128)(2,1)S(1)}, u32[]{:S(2)}, u32[]{:S(2)}) collective-permute-start(bf16[768,256]{1,0:T(8,128)(2,1)S(1)} %get-tuple-element.93), channel_id=1, source_target_pairs={{0,7},{1,6},{2,5},{3,4},{4,11},{5,10},{6,9},{7,8},{8,15},{9,14},{1... | collective-permute-start | bytes 1179656 | tf_op jit(solution)/shard_map/ppermute | solution.py:25
  334.0 51.2 %collective-permute-start.22 = (bf16[768,256]{1,0:T(8,128)(2,1)S(1)}, bf16[768,256]{1,0:T(8,128)(2,1)S(1)}, u32[]{:S(2)}, u32[]{:S(2)}) collective-permute-start(bf16[768,256]{1,0:T(8,128)(2,1)S(1)} %get-tuple-element.94), channel_id=1, source_target_pairs={{0,2},{1,3},{2,0},{3,1},{4,6},{5,7},{6,4},{7,5},{8,10},{9,11},{10,... | collective-permute-start | bytes 1179656 | tf_op jit(solution)/shard_map/ppermute | solution.py:25
  334.5 53.4 %collective-permute-start.23 = (bf16[768,256]{1,0:T(8,128)(2,1)S(1)}, bf16[768,256]{1,0:T(8,128)(2,1)S(1)}, u32[]{:S(2)}, u32[]{:S(2)}) collective-permute-start(bf16[768,256]{1,0:T(8,128)(2,1)S(1)} %get-tuple-element.95), channel_id=1, source_target_pairs={{0,3},{1,2},{2,1},{3,0},{4,7},{5,6},{6,5},{7,4},{8,11},{9,10},{10,... | collective-permute-start | bytes 1179656 | tf_op jit(solution)/shard_map/ppermute | solution.py:25
  (78 other events, 2590.9 us)
